TPU v7x, 256 devices: a whole 4x4x8 slice. The times are simulated.
256 devices in a mesh: space: 32 (over x, z), tile: 8 (over y, core).
Axes of the slice: x: 4, y: 4, z: 8, core: 2. Of those that a mesh axis runs over, the one named last changes fastest.
Arguments:
- eigenvectors: float32 [2, 256, 3, 262144], P(None, None, None, ('space', 'tile')), may hold values from -6 to 6
- perambulator: float32 [2, 1024, 1024], P(None, 'space'), may hold values from -6 to 6
- momenta: int32 [2, 3], replicated, may hold values from 1 to 2
- graph_blocks: int32 [256, 2], replicated, may hold values from 0 to 15
Outputs:
- elementals: float32 [2, 2, 256, 256], P(None, None, 'tile', 'space')
- contractions: float32 [256, 2, 128, 128], P(('space', 'tile'))
All inputs are finite; a program needn't handle non-finite values.
Results may differ from a plain program's by a relative error of at most 0.00016.
Values sent between devices are 32-bit elements; how exact they have to be, the bound alone decides.
A program may use at most 64 MiB of HBM per device.

v0:
```python
import math

import jax
import jax.numpy as jnp
from jax import lax
from jax.sharding import PartitionSpec as P

NEV = 256
NC = 3
SPIN = 4
NMOM = 2
EDGE = 64
HIGH = lax.Precision.HIGH


def gram(vectors, momenta, first_site):
    site = first_site + lax.iota(jnp.int32, vectors.shape[3])
    x, y, z = site % EDGE, site // EDGE % EDGE, site // (EDGE * EDGE)
    wave = (momenta[:, 0:1] * x + momenta[:, 1:2] * y + momenta[:, 2:3] * z) % EDGE
    angle = wave.astype(jnp.float32) * (2.0 * math.pi / EDGE)
    cosine, sine = jnp.cos(angle), jnp.sin(angle)
    real, imag = vectors[0], vectors[1]

    def dot(a, b):
        return lax.dot_general(
            a,
            b,
            (((1, 2), (1, 2)), ((), ())),
            precision=HIGH,
            preferred_element_type=jnp.float32,
        )

    out = []
    for p in range(NMOM):
        c, s = cosine[p][None, None, :], sine[p][None, None, :]
        pr = c * real + s * imag
        pi = c * imag - s * real
        rr = dot(real, pr)
        ii = dot(imag, pi)
        mixed = dot(real - imag, pr + pi)
        out.append(jnp.stack([rr + ii, mixed - rr + ii]))
    return jnp.stack(out)


def per_device(eigenvectors, perambulator, momenta, graph_blocks):
    tiles = lax.axis_size("tile")
    spaces = lax.axis_size("space")
    space, tile = lax.axis_index("space"), lax.axis_index("tile")
    sites = eigenvectors.shape[3]
    mine = space * tiles + tile
    norm = 1.0 / math.sqrt(NC * sites * spaces * tiles)
    tau = perambulator.reshape(2, -1, NEV, SPIN).transpose(0, 3, 1, 2)
    tau = lax.all_gather(tau, "space", axis=2, tiled=True)
    phi = lax.psum(gram(eigenvectors, momenta, mine * sites) * norm, ("space", "tile"))
    rows, cols = NEV // tiles, NEV // spaces
    elementals = lax.dynamic_slice(phi, (0, 0, tile * rows, space * cols), (NMOM, 2, rows, cols))
    pair = lax.dynamic_slice(graph_blocks, (mine, 0), (1, 2))[0]
    by_block = phi.reshape(NMOM, 2, tiles, rows, NEV).transpose(0, 2, 1, 3, 4).reshape(-1, 2, rows, NEV)
    picked = by_block[pair]

    def apply(tau_part, phi_part):
        return jnp.einsum(
            "akj,bij->bkia", tau_part, phi_part, precision=HIGH, preferred_element_type=jnp.float32
        )

    re = apply(tau[0], picked[:, 0]) - apply(tau[1], picked[:, 1])
    im = apply(tau[0], picked[:, 1]) + apply(tau[1], picked[:, 0])
    scale = 1.0 / math.sqrt(NEV)
    re = (re * scale).reshape(2, re.shape[1], -1)
    im = (im * scale).reshape(2, im.shape[1], -1)

    def contract(a, b):
        return lax.dot_general(
            a, b, (((0,), (0,)), ((), ())), precision=HIGH, preferred_element_type=jnp.float32
        )

    out_re = contract(re[0], re[1]) - contract(im[0], im[1])
    out_im = contract(re[0], im[1]) + contract(im[0], re[1])
    contractions = jnp.stack([out_re, out_im])[None] * (1.0 / math.sqrt(SPIN * NEV))
    return elementals, contractions


def solution(mesh):
    return jax.shard_map(
        per_device,
        mesh=mesh,
        in_specs=(P(None, None, None, ("space", "tile")), P(None, "space", None), P(), P()),
        out_specs=(P(None, None, "tile", "space"), P(("space", "tile"), None, None, None)),
        check_vma=False,
    )
```

profile of v0, /device:TPU:1, one launch (start us, length us, event | category | flops | bytes accessed | tf_op | source)
XLA Modules:
  0.0 337.6 jit_solution(6767682924456943467)
XLA Ops:
  8.1 1.0 slice_reduce_fusion.2
  9.5 5.6 %fusion.74 = f32[256,256]{0,1:T(8,128)S(1)} fusion(f32[2,256,3,1024]{3,1,2,0:T(8,128)} %param.4, f32[1024]{0:T(1024)S(1)} %bitcast.216, f32[1024]{0:T(1024)S(1)} %bitcast.213), kind=kOutput, calls=%fused_computation.66 | convolution fusion | flops 1210318848 | bytes 9707520 | tf_op jit(solution)/shard_map/dot_general | solution.py:25
  15.1 1.7 fusion.69
  16.9 2.2 fusion.109
  19.1 1.7 fusion.59
  20.9 1.7 fusion.54
  22.6 2.2 fusion.99
  25.1 1.1 maximum_multiply_fusion
  26.6 1.1 copy.14
  27.9 277.1 %all-reduce.2.cloned.1.call-done = f32[2,2,256,256]{2,3,1,0:T(8,128)} async-done(((f32[2,2,256,256]{2,3,1,0:T(8,128)}), f32[2,2,256,256]{2,3,1,0:T(8,128)}) %all-reduce.2.cloned.1.call-update) | async-done | bytes 1048592 | tf_op jit(solution)/shard_map/psum | solution.py:54
  305.0 1.6 copy.10
  306.7 0.6 gather_fusion
  307.3 1.4 constant_dynamic-slice_fusion
  308.7 4.2 %fusion = f32[2,32,4,1024]{3,1,2,0:T(8,128)S(1)} fusion(f32[2,4,1024,256]{3,2,1,0:T(8,128)} %all-gather.2.cloned.1.call-done, f32[2,2,32,256]{3,2,1,0:T(8,128)S(1)} %gather_fusion), kind=kOutput, calls=%fused_computation.3 | convolution fusion | flops 402653184 | bytes 5308416 | tf_op jit(solution)/shard_map/akj,bij->bkia/dot_general | solution.py:62
  312.9 4.2 %fusion.51 = f32[2,1024,32,4]{1,2,3,0:T(8,128)S(1)} fusion(f32[2,32,4,1024]{3,1,2,0:T(8,128)S(1)} %fusion, f32[2,4,1024,256]{3,2,1,0:T(8,128)} %all-gather.2.cloned.1.call-done, f32[2,2,32,256]{3,2,1,0:T(8,128)S(1)} %gather_fusion), kind=kOutput, calls=%fused_computation.59 | convolution fusion | flops 403177472 | bytes 6356992 | tf_op jit(solution)/shard_map/akj,bij->bkia/dot_general | solution.py:62
  317.2 0.3 copy.18
  317.8 0.3 copy.19
  318.3 4.2 %fusion.1 = f32[2,32,4,1024]{3,1,2,0:T(8,128)S(1)} fusion(f32[2,4,1024,256]{3,2,1,0:T(8,128)} %all-gather.2.cloned.1.call-done, f32[2,2,32,256]{3,2,1,0:T(8,128)S(1)} %gather_fusion), kind=kOutput, calls=%fused_computation.4 | convolution fusion | flops 402653184 | bytes 5308416 | tf_op jit(solution)/shard_map/akj,bij->bkia/dot_general | solution.py:62
  322.5 4.2 %fusion.53 = f32[2,1024,32,4]{1,2,3,0:T(8,128)S(1)} fusion(f32[2,32,4,1024]{3,1,2,0:T(8,128)S(1)} %fusion.1, f32[2,4,1024,256]{3,2,1,0:T(8,128)} %all-gather.2.cloned.1.call-done, f32[2,2,32,256]{3,2,1,0:T(8,128)S(1)} %gather_fusion), kind=kOutput, calls=%fused_computation.61 | convolution fusion | flops 403177472 | bytes 6356992 | tf_op jit(solution)/shard_map/akj,bij->bkia/dot_general | solution.py:62
  327.9 0.4 fusion.134
  328.3 0.4 fusion.133
  328.7 0.4 fusion.114
  329.1 0.4 fusion.115
  329.5 0.7 maximum_multiply_fusion.1
  (34 shorter events, 3.0 us)
Async XLA Ops:
  8.0 19.7 %copy-start = (s32[256,2]{0,1:T(2,128)S(1)}, s32[256,2]{0,1:T(2,128)}, u32[]{:S(2)}) copy-start(s32[256,2]{0,1:T(2,128)} %param.7) | copy-start | bytes 6148
  8.0 297.0 %all-reduce.2.cloned.1.call-start = ((), (), s32[]{:S(2)}) async-start(), calls=%async_computation | async-start | bytes 2097152 | tf_op jit(solution)/shard_map/psum | solution.py:54
  9.5 5.6 %copy-start.1 = (f32[2,256,3,1024]{3,1,2,0:T(8,128)S(1)}, f32[2,256,3,1024]{3,1,2,0:T(8,128)}, u32[]{:S(2)}) copy-start(f32[2,256,3,1024]{3,1,2,0:T(8,128)} %param.4) | copy-start | bytes 18874372
  24.8 1.5 copy-start.2
  26.2 282.5 %all-gather.2.cloned.1.call-start = ((), (), s32[]{:S(2)}) async-start(), calls=%async_computation.1 | async-start | bytes 8650752 | tf_op jit(solution)/shard_map/all_gather | solution.py:53
Sparse Core Ops, SparseCore 0:
  26.4 278.6 all-reduce.1
Sparse Core Ops, SparseCore 1:
  29.3 100.9 all-gather.1
where the time goes:
time: 339 us; the launch traced here: 338 us
  waiting for transfers between devices  277 us (82%)
  matrix products  33.7 us (10%)
  between operations  15.8 us (5%)
  local copies, waits for them, and re-layouts  8.6 us (3%)
    psum x1, waiting for transfers between devices, per_device(): lax.psum(gram(eigenvectors, momenta, mine * sites) * norm, ('space', 'til...  277 us
    dot_general x4, matrix products, apply(): jnp.einsum('akj,bij->bkia', tau_part, phi_part, precision=HIGH, preferred...  16.9 us
    dot_general x6, matrix products, dot(): lax.dot_general(a, b, (((1, 2), (1, 2)), ((), ())), precision=HIGH, prefe...  15.2 us
  transfers between devices with their start and end apart: 2, of which 1 were waited for; matrix products, arithmetic and copies ran while one was open for 2% of the time, Pallas kernels for 0%

commit v1 on v0

v1 whole, which is shorter than its diff:
```python
import functools
import math

import jax
import jax.numpy as jnp
from jax import lax
from jax.experimental import pallas as pl
from jax.experimental.pallas import tpu as pltpu
from jax.sharding import PartitionSpec as P

NEV = 256
NC = 3
SPIN = 4
NMOM = 2
EDGE = 64
NX, NY, NZ = 4, 4, 8
PLANE = NX * NY
RANKS = 2 * PLANE
NSPACE = NX * NZ
MESH = pl.DeviceIdType.MESH
F32 = jnp.float32
BF16 = jnp.bfloat16
NT = (((1,), (1,)), ((), ()))
TN = (((0,), (0,)), ((), ()))


def split(v):
    hi = v.astype(BF16)
    return hi, (v - hi.astype(F32)).astype(BF16)


def dot(a, b, dims=NT):
    return lax.dot_general(a, b, dims, preferred_element_type=F32)


def kernel(
    momenta, graphs, eig, tau_in, el_ref, out_ref,
    vec, left, trig, acc, ebuf, stage, pair_in, plane_in, line_in, full, pick, picked, rows, rowed,
    tau, tau_hi, tau_lo,
    load_sem, own_sem, pair_send, pair_recv, plane_send, plane_recv, line_send, line_recv,
    pick_send, pick_recv, rows_send, rows_recv,
    ax_send, ax_recv, az_send, az_recv, bz_send, bz_recv, bx_send, bx_recv, push_send, push_recv,
):
    space, tile = lax.axis_index("space"), lax.axis_index("tile")
    x, z = space // NZ, space % NZ
    y, core = tile // 2, tile % 2
    place = x * NY + y
    rank = core * PLANE + place
    me = space * (2 * NY) + tile
    sites = vec.shape[3]

    def at_plane(other_rank):
        c, q = other_rank // PLANE, other_rank % PLANE
        return ((q // NY) * NZ + z, (q % NY) * 2 + c)

    def at_z(zz):
        return (x * NZ + zz, tile)

    def at_x(xx):
        return (xx * NZ + z, tile)

    partner = (space, y * 2 + 1 - core)

    def remote(src, dst, send, recv, device):
        return pltpu.make_async_remote_copy(
            src_ref=src, dst_ref=dst, send_sem=send, recv_sem=recv, device_id=device, device_id_type=MESH
        )

    barrier = pltpu.get_barrier_semaphore()

    def greet(j, _):
        pl.semaphore_signal(barrier, inc=1, device_id=at_plane((rank + j) % RANKS), device_id_type=MESH)
        return 0

    lax.fori_loop(1, RANKS, greet, 0)

    def greet_z(j, _):
        pl.semaphore_signal(barrier, inc=1, device_id=at_z((z + j) % NZ), device_id_type=MESH)
        return 0

    lax.fori_loop(1, NZ, greet_z, 0)

    loads = [pltpu.make_async_copy(eig.at[:, c], vec.at[:, c], load_sem.at[c]) for c in range(NC)]
    for load in loads:
        load.start()
    a_a, a_b = 2 * core, 2 * core + 1
    slot = z * NX + x
    own = [
        pltpu.make_async_copy(tau_in.at[a_a], tau.at[a_a, slot], own_sem.at[0]),
        pltpu.make_async_copy(tau_in.at[a_b], tau.at[a_b, slot], own_sem.at[1]),
    ]
    for copy in own:
        copy.start()

    site = me * sites + lax.broadcasted_iota(jnp.int32, (1, sites), 1)
    px, py, pz = site & (EDGE - 1), (site >> 6) & (EDGE - 1), site >> 12
    for p in range(NMOM):
        wave = (momenta[p, 0] * px + momenta[p, 1] * py + momenta[p, 2] * pz) & (EDGE - 1)
        angle = wave.astype(F32) * (2.0 * math.pi / EDGE)
        trig[p, 0:1, :] = jnp.cos(angle)
        trig[p, 1:2, :] = jnp.sin(angle)

    pl.semaphore_wait(barrier, RANKS - 1 + NZ - 1)

    started = []

    def go(copy):
        copy.start()
        started.append(copy)

    def bundle(a, zz):
        return tau.at[a, pl.ds(zz * NX, NX)]

    def half_bundle(a, zz, h):
        return tau.at[a, pl.ds(zz * NX + h * (NX // 2), NX // 2)]

    def push(a, zz, k):
        go(remote(bundle(a, zz), bundle(a, zz), push_send.at[k], push_recv.at[k], partner))

    def waits(ref, sem):
        pltpu.make_async_copy(ref, ref, sem).wait()

    def b_along_x(zz, k):
        for j in range(1, NX):
            ref = tau.at[a_b, zz * NX + x]
            go(remote(ref, ref, bx_send.at[k, j - 1], bx_recv.at[k], at_x((x + j) % NX)))

    def z_back(h):
        return (z + NZ - h) % NZ

    def z_on(h):
        return (z + h) % NZ

    def tau_first():
        own[0].wait()
        own[1].wait()
        for j in range(1, NX):
            ref = tau.at[a_a, slot]
            go(remote(ref, ref, ax_send.at[j - 1], ax_recv.at[0], at_x((x + j) % NX)))
        ref = tau.at[a_b, slot]
        go(remote(ref, ref, bz_send.at[0, 0], bz_recv.at[0, 0], at_z(z_on(1))))
        go(remote(ref, ref, bz_send.at[1, 0], bz_recv.at[1, 0], at_z(z_back(1))))
        b_along_x(z, 0)

    def b_z(h):
        up, down = z_back(h), z_on(h)
        ref_up, ref_down = tau.at[a_b, up * NX + x], tau.at[a_b, down * NX + x]
        if h < NZ // 2:
            waits(ref_up, bz_recv.at[0, h - 1])
            waits(ref_down, bz_recv.at[1, h - 1])
            if h + 1 == NZ // 2:
                ref_u, ref_d = ref_up.at[0], ref_down.at[1]
            else:
                ref_u, ref_d = ref_up, ref_down
            go(remote(ref_u, ref_u, bz_send.at[0, h], bz_recv.at[0, h], at_z(z_on(1))))
            go(remote(ref_d, ref_d, bz_send.at[1, h], bz_recv.at[1, h], at_z(z_back(1))))
            b_along_x(up, h)
            b_along_x(down, NZ // 2 + h)
        else:
            waits(ref_up.at[0], bz_recv.at[0, h - 1])
            waits(ref_up.at[1], bz_recv.at[1, h - 1])
            b_along_x(up, h)

    def b_push(k):
        zz = z_back(k) if k <= NZ // 2 else z_on(k - NZ // 2)
        waits(tau.at[a_b, pl.ds(0, NX - 1)], bx_recv.at[k])
        push(a_b, zz, NZ + k)

    def a_z(h):
        up, down = z_back(h), z_on(h)
        if h == 0:
            waits(tau.at[a_a, pl.ds(0, NX - 1)], ax_recv.at[0])
            go(remote(bundle(a_a, z), bundle(a_a, z), az_send.at[0, 0], az_recv.at[0, 0], at_z(z_on(1))))
            go(remote(bundle(a_a, z), bundle(a_a, z), az_send.at[1, 0], az_recv.at[1, 0], at_z(z_back(1))))
            push(a_a, z, 0)
        elif h < NZ // 2:
            waits(bundle(a_a, up), az_recv.at[0, h - 1])
            waits(bundle(a_a, down), az_recv.at[1, h - 1])
            if h + 1 == NZ // 2:
                ref_u, ref_d = half_bundle(a_a, up, 0), half_bundle(a_a, down, 1)
            else:
                ref_u, ref_d = bundle(a_a, up), bundle(a_a, down)
            go(remote(ref_u, ref_u, az_send.at[0, h], az_recv.at[0, h], at_z(z_on(1))))
            go(remote(ref_d, ref_d, az_send.at[1, h], az_recv.at[1, h], at_z(z_back(1))))
            push(a_a, up, h)
            push(a_a, down, NZ // 2 + h)
        else:
            waits(half_bundle(a_a, up, 0), az_recv.at[0, h - 1])
            waits(half_bundle(a_a, up, 1), az_recv.at[1, h - 1])
            push(a_a, up, h)

    width = 512

    def gram(p, c):
        def body(b, _):
            cols = pl.ds(pl.multiple_of(b * width, width), width)
            r, i = vec[0, c, :, cols], vec[1, c, :, cols]
            co, si = trig[p, 0:1, cols], trig[p, 1:2, cols]
            wr = co * r + si * i
            wi = co * i - si * r
            for k, (lhs, rhs) in enumerate(((r, wr), (i, wi), (None, wr + wi))):
                if p == 0:
                    lh, ll = split(r - i if lhs is None else lhs)
                    left[k, 0, c, :, cols] = lh
                    left[k, 1, c, :, cols] = ll
                else:
                    lh, ll = left[k, 0, c, :, cols], left[k, 1, c, :, cols]
                rh, rl = split(rhs)
                acc[k] += dot(lh, rh) + dot(lh, rl) + dot(ll, rh)
            return 0

        lax.fori_loop(0, sites // width, body, 0)

    norm = 1.0 / math.sqrt(NC * sites * NSPACE * 2 * NY)

    def pair_copy(p):
        return remote(stage.at[p, 1 - core], pair_in.at[p], pair_send.at[p], pair_recv.at[p], partner)

    def finish_gram(p):
        p1, p2, p3 = acc[0], acc[1], acc[2]
        for ri, part in enumerate((p1 + p2, p3 - p1 + p2)):
            part = part * norm
            ebuf[ri, 0] = part[:, :128]
            ebuf[ri, 1] = part[:, 128:]
        for r in range(RANKS):
            for ri in range(2):
                for h in range(2):
                    lanes = pl.ds(h * 128, 128)
                    stage[p, r // PLANE, r % PLANE, ri, :, lanes] = ebuf[ri, h, pl.ds(r, 8, stride=32), :]
        go(pair_copy(p))

    def plane_stage(p):
        pair_copy(p).wait_recv()
        stage[p, core] += pair_in[p]

        def send(j, _):
            q = (place + j) % PLANE
            remote(
                stage.at[p, core, q], plane_in.at[p, place], plane_send.at[p], plane_recv.at[p],
                at_plane(core * PLANE + q),
            ).start()
            return 0

        lax.fori_loop(1, PLANE, send, 0)
        plane_in[p, place] = stage[p, core, place]

    def line_stage(p):
        waits(plane_in.at[p, pl.ds(0, PLANE - 1)], plane_recv.at[p])
        total = plane_in[p, 0]
        for q in range(1, PLANE):
            total = total + plane_in[p, q]
        line_in[p, z] = total

        def send(j, _):
            ref = line_in.at[p, z]
            remote(ref, ref, line_send.at[p], line_recv.at[p], at_z((z + j) % NZ)).start()
            return 0

        lax.fori_loop(1, NZ, send, 0)

    def full_stage(p):
        waits(line_in.at[p, pl.ds(0, NZ - 1)], line_recv.at[p])
        total = line_in[p, 0]
        for q in range(1, NZ):
            total = total + line_in[p, q]
        for ri in range(2):
            full[ri, p * 8 : p * 8 + 8, :] = total[ri]

    def pick_stage():
        def fill(d, _):
            sp, tl = at_plane(d)
            g = sp * (2 * NY) + tl
            u, v = graphs[g, 0], graphs[g, 1]
            for k, (block, ri) in enumerate(((u, 0), (u, 1), (v, 0), (v, 1))):
                pick[d, k : k + 1, :] = full[ri, pl.ds(block, 1), :]
            return 0

        lax.fori_loop(0, RANKS, fill, 0)

        def send(j, _):
            d = (rank + j) % RANKS
            remote(pick.at[d], picked.at[rank], pick_send.at[0], pick_recv.at[0], at_plane(d)).start()
            return 0

        lax.fori_loop(1, RANKS, send, 0)
        picked[rank] = pick[rank]

        def fill_rows(d, _):
            _, tl = at_plane(d)
            for k in range(4):
                rows[d, k : k + 1, :] = full[k % 2, pl.ds((k // 2) * 8 + tl, 1), :]
            return 0

        lax.fori_loop(0, RANKS, fill_rows, 0)

        def send_rows(j, _):
            d = (rank + j) % RANKS
            remote(rows.at[d], rowed.at[rank], rows_send.at[0], rows_recv.at[0], at_plane(d)).start()
            return 0

        lax.fori_loop(1, RANKS, send_rows, 0)
        rowed[rank] = rows[rank]

    def convert(a):
        def body(s, _):
            for ri in range(2):
                hi, lo = split(tau[a, s, ri])
                where = pl.ds(pl.multiple_of(s * 32, 32), 32)
                tau_hi[a, ri, where, :] = hi
                tau_lo[a, ri, where, :] = lo
            return 0

        lax.fori_loop(0, NSPACE, body, 0)

    def final():
        waits(picked.at[pl.ds(0, RANKS - 1)], pick_recv.at[0])
        u_re, u_im, v_re, v_im = (picked[:, k, :] for k in range(4))
        scale = 1.0 / math.sqrt(NEV)
        b_re = jnp.concatenate([u_re, u_im, v_re, v_im], axis=0) * scale
        b_im = jnp.concatenate([-u_im, u_re, -v_im, v_re], axis=0) * scale
        re_hi, re_lo = split(b_re)
        im_hi, im_lo = split(b_im)
        re_both = jnp.concatenate([re_hi, re_lo], axis=0)
        im_both = jnp.concatenate([im_hi, im_lo], axis=0)
        us, vs = [], []
        for a in range(SPIN):
            wide = dot(tau_hi[a, 0], re_both) + dot(tau_hi[a, 1], im_both)
            thin = dot(tau_lo[a, 0], re_hi) + dot(tau_lo[a, 1], im_hi)
            r = wide[:, :128] + wide[:, 128:] + thin
            us.append(r[:, :64])
            vs.append(r[:, 64:])
        u_all = jnp.concatenate(us, axis=1)
        v_all = jnp.concatenate(vs, axis=1)
        uh, ul = split(u_all)
        vh, vl = split(v_all)
        c4 = dot(uh, vh, TN) + dot(uh, vl, TN) + dot(ul, vh, TN)
        ii = lax.broadcasted_iota(jnp.int32, (128, NEV), 0)
        jj = lax.broadcasted_iota(jnp.int32, (128, NEV), 1)
        from_re = (jj == (ii % 4) * 64 + ii // 4).astype(F32)
        from_im = (jj == (ii % 4) * 64 + 32 + ii // 4).astype(F32)

        def exact(a, b, dims):
            return lax.dot_general(a, b, dims, precision=lax.Precision.HIGHEST, preferred_element_type=F32)

        nn = (((1,), (0,)), ((), ()))
        top = exact(from_re, c4, nn)
        low = exact(from_im, c4, nn)
        scale2 = 1.0 / math.sqrt(SPIN * NEV)
        out_ref[0] = (exact(top, from_re, NT) - exact(low, from_im, NT)) * scale2
        out_ref[1] = (exact(top, from_im, NT) + exact(low, from_re, NT)) * scale2

    def elementals():
        waits(rowed.at[pl.ds(0, RANKS - 1)], rows_recv.at[0])
        width8 = NEV // NSPACE
        for k in range(4):
            turned = pltpu.roll(rowed[:, k, :], (NEV - space * width8) % NEV, 1)
            el_ref[k // 2, k % 2] = turned[:, :width8]

    tau_first()
    acc[...] = jnp.zeros_like(acc)
    loads[0].wait()
    gram(0, 0)
    a_z(0)
    b_z(1)
    loads[1].wait()
    gram(0, 1)
    b_z(2)
    b_push(0)
    loads[2].wait()
    gram(0, 2)
    finish_gram(0)
    acc[...] = jnp.zeros_like(acc)
    b_z(3)
    gram(1, 0)
    plane_stage(0)
    a_z(1)
    b_push(1)
    b_push(5)
    gram(1, 1)
    b_z(4)
    gram(1, 2)
    finish_gram(1)
    line_stage(0)
    plane_stage(1)
    a_z(2)
    b_push(2)
    b_push(6)
    b_push(3)
    b_push(7)
    b_push(4)
    line_stage(1)
    full_stage(0)
    a_z(3)
    full_stage(1)
    a_z(4)
    pick_stage()
    for k in range(2 * NZ):
        waits(tau.at[0, pl.ds(0, NX)], push_recv.at[k])
    for a in range(SPIN):
        convert(a)
    final()
    elementals()
    for copy in started:
        copy.wait_send()
    for p in range(NMOM):
        waits(plane_in.at[p, pl.ds(0, PLANE - 1)], plane_send.at[p])
        waits(line_in.at[p, pl.ds(0, NZ - 1)], line_send.at[p])
    waits(picked.at[pl.ds(0, RANKS - 1)], pick_send.at[0])
    waits(rowed.at[pl.ds(0, RANKS - 1)], rows_send.at[0])


def per_device(eigenvectors, perambulator, momenta, graph_blocks):
    sites = eigenvectors.shape[3]
    eig = eigenvectors.transpose(0, 2, 1, 3)
    tau_in = perambulator.reshape(2, -1, NEV, SPIN).transpose(3, 0, 1, 2)
    sources = tau_in.shape[2]
    dma = pltpu.SemaphoreType.DMA
    el, out = pl.pallas_call(
        kernel,
        out_shape=(
            jax.ShapeDtypeStruct((NMOM, 2, 32, NEV // NSPACE), F32),
            jax.ShapeDtypeStruct((2, 128, 128), F32),
        ),
        in_specs=[
            pl.BlockSpec(memory_space=pltpu.SMEM),
            pl.BlockSpec(memory_space=pltpu.SMEM),
            pl.BlockSpec(memory_space=pl.ANY),
            pl.BlockSpec(memory_space=pltpu.VMEM),
        ],
        out_specs=(pl.BlockSpec(memory_space=pltpu.VMEM), pl.BlockSpec(memory_space=pltpu.VMEM)),
        scratch_shapes=[
            pltpu.VMEM((2, NC, NEV, sites), F32),
            pltpu.VMEM((3, 2, NC, NEV, sites), BF16),
            pltpu.VMEM((NMOM, 2, sites), F32),
            pltpu.VMEM((3, NEV, NEV), F32),
            pltpu.VMEM((2, 2, NEV, 128), F32),
            pltpu.VMEM((NMOM, 2, PLANE, 2, 8, NEV), F32),
            pltpu.VMEM((NMOM, PLANE, 2, 8, NEV), F32),
            pltpu.VMEM((NMOM, PLANE, 2, 8, NEV), F32),
            pltpu.VMEM((NMOM, NZ, 2, 8, NEV), F32),
            pltpu.VMEM((2, 16, NEV), F32),
            pltpu.VMEM((RANKS, 4, NEV), F32),
            pltpu.VMEM((RANKS, 4, NEV), F32),
            pltpu.VMEM((RANKS, 4, NEV), F32),
            pltpu.VMEM((RANKS, 4, NEV), F32),
            pltpu.VMEM((SPIN, NSPACE, 2, sources, NEV), F32),
            pltpu.VMEM((SPIN, 2, NSPACE * sources, NEV), BF16),
            pltpu.VMEM((SPIN, 2, NSPACE * sources, NEV), BF16),
            dma((NC,)),
            dma((2,)),
            dma((NMOM,)),
            dma((NMOM,)),
            dma((NMOM,)),
            dma((NMOM,)),
            dma((NMOM,)),
            dma((NMOM,)),
            dma((1,)),
            dma((1,)),
            dma((1,)),
            dma((1,)),
            dma((NX - 1,)),
            dma((1,)),
            dma((2, NZ // 2)),
            dma((2, NZ // 2)),
            dma((2, NZ // 2)),
            dma((2, NZ // 2)),
            dma((NZ, NX - 1)),
            dma((NZ,)),
            dma((2 * NZ,)),
            dma((2 * NZ,)),
        ],
        compiler_params=pltpu.CompilerParams(
            collective_id=0, has_side_effects=True, vmem_limit_bytes=60 * 2**20
        ),
    )(momenta, graph_blocks, eig, tau_in)
    return el, out[None]


def solution(mesh):
    return jax.shard_map(
        per_device,
        mesh=mesh,
        in_specs=(P(None, None, None, ("space", "tile")), P(None, "space", None), P(), P()),
        out_specs=(P(None, None, "tile", "space"), P(("space", "tile"), None, None, None)),
        check_vma=False,
    )
```

time: 339 us -> 81.4 us (0.24)
  waiting for transfers between devices: 277 us -> 0 us
  Pallas kernels: 0 us -> 73.6 us
  matrix products: 33.7 us -> 0 us
  between operations: 15.8 us -> 0.65 us
    psum x1 -> x0, waiting for transfers between devices: 277 us -> none  [per_device(): lax.psum(gram(eigenvectors, momenta, mine * sites) * norm, ('space', 'til...]
    pallas_call x0 -> x1, Pallas kernels: none -> 73.6 us  [per_device(): pl.pallas_call(kernel, out_shape=(jax.ShapeDtypeStruct((NMOM, 2, 32, NEV...]
    dot_general x14 -> x0, matrix products: 33.7 us -> none  [the longest x4 16.9 us: apply(): jnp.einsum('akj,bij->bkia', tau_part, phi_part, precision=HIGH, preferred...]
    unnamed x7 -> x4, local copies, waits for them, and re-layouts: 0.35 us -> 5.84 us
  transfers between devices with their start and end apart: 2 -> 0, of which waited for: 1 -> 0; matrix products, arithmetic and copies ran while one was open for 2% -> 0% of each run, Pallas kernels for 0% -> 0%
where the time goes in v1:
time: 81.4 us; the launch traced here: 81.1 us
  Pallas kernels  73.6 us (90%)
  local copies, waits for them, and re-layouts  6.88 us (8%)
    pallas_call x1, Pallas kernels, per_device(): pl.pallas_call(kernel, out_shape=(jax.ShapeDtypeStruct((NMOM, 2, 32, NEV...  73.6 us
    unnamed x4, local copies, waits for them, and re-layouts  5.84 us

profile of v1, /device:TPU:1, one launch (start us, length us, event | category | flops | bytes accessed | tf_op | source)
XLA Modules:
  0.0 81.1 jit_solution(10484045427857161329)
XLA Ops:
  0.6 1.3 %copy.8 = f32[2,32,1024]{1,2,0:T(8,128)S(1)} copy(f32[2,32,1024]{2,1,0:T(8,128)} %param.5) | data formatting | bytes 524288 | tf_op args[1]
  1.9 1.0 %copy.9 = f32[2,32,256,4]{2,1,0,3:T(8,128)} copy(f32[2,32,256,4]{1,3,2,0:T(4,128)S(1)} %bitcast.5) | data formatting | bytes 524288 | tf_op jit(solution)/shard_map/reshape | solution.py:415
  3.0 1.5 %copy.10.graphs = s32[256,2]{1,0:T(8,128)} copy(s32[256,2]{0,1:T(2,128)} %param.7) | data formatting | bytes 4096 | tf_op args[3]
  4.4 73.6 %shard_map.59 = (f32[2,2,32,8]{3,2,1,0:T(8,128)}, f32[2,128,128]{2,1,0:T(8,128)}) custom-call(s32[2,3]{1,0:T(2,128)} %momenta.1, s32[256,2]{1,0:T(8,128)} %copy.10.graphs, f32[2,3,256,1024]{3,2,1,0:T(8,128)} %bitcast.4, f32[4,2,32,256]{3,2,1,0:T(8,128)} %bitcast.6), custom_call_target="tpu_custom_call" | custom-call | tf_op jit(solution)/shard_map/pallas_call | solution.py:418
  78.1 1.5 %copy.11 = f32[2,2,32,8]{2,3,1,0:T(8,128)} copy(f32[2,2,32,8]{3,2,1,0:T(8,128)} %get-tuple-element.8) | data formatting | bytes 8192
  79.6 1.6 %copy.13 = f32[1,2,128,128]{3,2,1,0:T(8,128)} copy(f32[1,2,128,128]{3,2,1,0:T(8,128)} %bitcast.7) | data formatting | bytes 262144

commit v2 on v1

v2 whole, which is shorter than its diff:
```python
import functools
import math

import jax
import jax.numpy as jnp
from jax import lax
from jax.experimental import pallas as pl
from jax.experimental.pallas import tpu as pltpu
from jax.sharding import PartitionSpec as P

NEV = 256
NC = 3
SPIN = 4
NMOM = 2
EDGE = 64
NX, NY, NZ = 4, 4, 8
PLANE = NX * NY
RANKS = 2 * PLANE
NSPACE = NX * NZ
BLOCK = 128
KDEV = 16
MESH = pl.DeviceIdType.MESH
F32 = jnp.float32
BF16 = jnp.bfloat16
NT = (((1,), (1,)), ((), ()))
TN = (((0,), (0,)), ((), ()))


def split(v):
    hi = v.astype(BF16)
    return hi, (v - hi.astype(F32)).astype(BF16)


def dot(a, b, dims=NT):
    return lax.dot_general(a, b, dims, preferred_element_type=F32)


def kernel(
    momenta_in, graphs_in, eig, sources_in, el_out, own_out, other_out,
    momenta, graphs, sources, el_ref, own_ref, vec, left, trig, acc, ebuf, stage, pair_in, plane_in, line_in, full, pick, picked, rows, rowed,
    tau_in, tau, tau_hi, tau_lo, foreign,
    load_sem, own_sem, pair_send, pair_recv, plane_send, plane_recv, line_send, line_recv,
    pick_send, pick_recv, rows_send, rows_recv,
    ax_send, ax_recv, az_send, az_recv, bz_send, bz_recv, bx_send, bx_recv, push_send, push_recv, swap_send, swap_recv, small_sem, out_sem,
):
    space, tile = lax.axis_index("space"), lax.axis_index("tile")
    x, z = space // NZ, space % NZ
    y, core = tile // 2, tile % 2
    place = x * NY + y
    rank = core * PLANE + place
    me = space * (2 * NY) + tile
    sites = vec.shape[3]

    def at_plane(other_rank):
        c, q = other_rank // PLANE, other_rank % PLANE
        return ((q // NY) * NZ + z, (q % NY) * 2 + c)

    def at_z(zz):
        return (x * NZ + zz, tile)

    def at_x(xx):
        return (xx * NZ + z, tile)

    partner = (space, y * 2 + 1 - core)

    def remote(src, dst, send, recv, device):
        return pltpu.make_async_remote_copy(
            src_ref=src, dst_ref=dst, send_sem=send, recv_sem=recv, device_id=device, device_id_type=MESH
        )

    small = [
        pltpu.make_async_copy(momenta_in, momenta, small_sem.at[0]),
        pltpu.make_async_copy(sources_in, sources, small_sem.at[1]),
        pltpu.make_async_copy(graphs_in, graphs, small_sem.at[2]),
    ]
    for copy in small:
        copy.start()
    loads = [pltpu.make_async_copy(eig.at[:, c], vec.at[:, c], load_sem.at[c]) for c in range(NC)]
    for load in loads:
        load.start()

    barrier = pltpu.get_barrier_semaphore()

    for j in range(1, RANKS):
        pl.semaphore_signal(barrier, inc=1, device_id=at_plane((rank + j) % RANKS), device_id_type=MESH)
    for j in range(1, NZ):
        pl.semaphore_signal(barrier, inc=1, device_id=at_z((z + j) % NZ), device_id_type=MESH)

    a_a, a_b = 2 * core, 2 * core + 1
    slot = z * NX + x

    def phases():
        site = me * sites + 128 * lax.broadcasted_iota(jnp.int32, (8, 128), 0)
        site = site + lax.broadcasted_iota(jnp.int32, (8, 128), 1)
        px, py, pz = site & (EDGE - 1), (site >> 6) & (EDGE - 1), site >> 12
        for p in range(NMOM):
            wave = (momenta[p, 0] * px + momenta[p, 1] * py + momenta[p, 2] * pz) & (EDGE - 1)
            angle = wave.astype(F32) * (2.0 * math.pi / EDGE)
            for k, value in enumerate((jnp.cos(angle), jnp.sin(angle))):
                for row in range(8):
                    trig[p, k : k + 1, row * 128 : row * 128 + 128] = value[row : row + 1, :]

    def spread():
        half = SPIN * 128
        jj = lax.broadcasted_iota(jnp.int32, (half, half), 0)
        col = lax.broadcasted_iota(jnp.int32, (half, half), 1)
        ones = (((jj & 3) * 128 + (jj >> 2)) == col).astype(F32).astype(BF16)
        first = pl.multiple_of((y % 2) * KDEV, KDEV)
        for h in range(2):
            lanes = slice(h * half, (h + 1) * half)
            value = jnp.concatenate([sources[0, pl.ds(first, KDEV), lanes], sources[1, pl.ds(first, KDEV), lanes]], axis=0)
            hi = value.astype(BF16)
            rest = value - hi.astype(F32)
            mid = rest.astype(BF16)
            low = (rest - mid.astype(F32)).astype(BF16)
            nn = (((1,), (0,)), ((), ()))
            parts = dot(jnp.concatenate([hi, mid, low], axis=0), ones, nn)
            n = 2 * KDEV
            moved = parts[:n] + parts[n : 2 * n] + parts[2 * n :]
            for a in range(SPIN):
                for ri in range(2):
                    tau_in[a, ri, :, h * 128 : h * 128 + 128] = moved[
                        ri * KDEV : (ri + 1) * KDEV, a * 128 : a * 128 + 128
                    ]

    started = []

    def go(copy):
        copy.start()
        started.append(copy)

    def bundle(a, zz):
        return tau.at[a, pl.ds(zz * NX, NX)]

    def half_bundle(a, zz, h):
        return tau.at[a, pl.ds(zz * NX + h * (NX // 2), NX // 2)]

    def push(a, zz, k):
        go(remote(bundle(a, zz), bundle(a, zz), push_send.at[k], push_recv.at[k], partner))

    def waits(ref, sem):
        pltpu.make_async_copy(ref, ref, sem).wait()

    def b_along_x(zz, k):
        for j in range(1, NX):
            ref = tau.at[a_b, zz * NX + x]
            go(remote(ref, ref, bx_send.at[k, j - 1], bx_recv.at[k], at_x((x + j) % NX)))

    def z_back(h):
        return (z + NZ - h) % NZ

    def z_on(h):
        return (z + h) % NZ

    def tau_first():
        own = [
            pltpu.make_async_copy(tau_in.at[a_a], tau.at[a_a, slot], own_sem.at[0]),
            pltpu.make_async_copy(tau_in.at[a_b], tau.at[a_b, slot], own_sem.at[1]),
        ]
        for copy in own:
            copy.start()
        for copy in own:
            copy.wait()
        for j in range(1, NX):
            ref = tau.at[a_a, slot]
            go(remote(ref, ref, ax_send.at[j - 1], ax_recv.at[0], at_x((x + j) % NX)))
        ref = tau.at[a_b, slot]
        go(remote(ref, ref, bz_send.at[0, 0], bz_recv.at[0, 0], at_z(z_on(1))))
        go(remote(ref, ref, bz_send.at[1, 0], bz_recv.at[1, 0], at_z(z_back(1))))

    def b_z(h):
        up, down = z_back(h), z_on(h)
        ref_up, ref_down = tau.at[a_b, up * NX + x], tau.at[a_b, down * NX + x]
        if h < NZ // 2:
            waits(ref_up, bz_recv.at[0, h - 1])
            waits(ref_down, bz_recv.at[1, h - 1])
            if h + 1 == NZ // 2:
                ref_u, ref_d = ref_up.at[0], ref_down.at[1]
            else:
                ref_u, ref_d = ref_up, ref_down
            go(remote(ref_u, ref_u, bz_send.at[0, h], bz_recv.at[0, h], at_z(z_on(1))))
            go(remote(ref_d, ref_d, bz_send.at[1, h], bz_recv.at[1, h], at_z(z_back(1))))
            b_along_x(up, h)
            b_along_x(down, NZ // 2 + h)
        else:
            waits(ref_up.at[0], bz_recv.at[0, h - 1])
            waits(ref_up.at[1], bz_recv.at[1, h - 1])
            b_along_x(up, h)

    def b_push(k):
        zz = z_back(k) if k <= NZ // 2 else z_on(k - NZ // 2)
        waits(tau.at[a_b, pl.ds(0, NX - 1)], bx_recv.at[k])
        push(a_b, zz, NZ + k)

    def a_z(h):
        up, down = z_back(h), z_on(h)
        if h == 0:
            waits(tau.at[a_a, pl.ds(0, NX - 1)], ax_recv.at[0])
            go(remote(bundle(a_a, z), bundle(a_a, z), az_send.at[0, 0], az_recv.at[0, 0], at_z(z_on(1))))
            go(remote(bundle(a_a, z), bundle(a_a, z), az_send.at[1, 0], az_recv.at[1, 0], at_z(z_back(1))))
            push(a_a, z, 0)
        elif h < NZ // 2:
            waits(bundle(a_a, up), az_recv.at[0, h - 1])
            waits(bundle(a_a, down), az_recv.at[1, h - 1])
            if h + 1 == NZ // 2:
                ref_u, ref_d = half_bundle(a_a, up, 0), half_bundle(a_a, down, 1)
            else:
                ref_u, ref_d = bundle(a_a, up), bundle(a_a, down)
            go(remote(ref_u, ref_u, az_send.at[0, h], az_recv.at[0, h], at_z(z_on(1))))
            go(remote(ref_d, ref_d, az_send.at[1, h], az_recv.at[1, h], at_z(z_back(1))))
            push(a_a, up, h)
            push(a_a, down, NZ // 2 + h)
        else:
            waits(half_bundle(a_a, up, 0), az_recv.at[0, h - 1])
            waits(half_bundle(a_a, up, 1), az_recv.at[1, h - 1])
            push(a_a, up, h)

    width = 512

    def gram(p, step):
        c, b = step // 2, step % 2
        cols = slice(b * width, (b + 1) * width)
        r, i = vec[0, c, :, cols], vec[1, c, :, cols]
        co, si = trig[p, 0:1, cols], trig[p, 1:2, cols]
        wr = co * r + si * i
        wi = co * i - si * r
        for k, (lhs, rhs) in enumerate(((r, wr), (i, wi), (None, wr + wi))):
            if p == 0:
                lh, ll = split(r - i if lhs is None else lhs)
                left[k, c, :NEV, cols] = lh
                left[k, c, NEV:, cols] = ll
            else:
                lh, ll = left[k, c, :NEV, cols], left[k, c, NEV:, cols]
            rh, rl = split(rhs)
            new = dot(lh, rh) + dot(lh, rl) + dot(ll, rh)
            if step == 0:
                acc[k] = new
            else:
                acc[k] += new

    def pair_copy(p):
        return remote(stage.at[p, 1 - core], pair_in.at[p], pair_send.at[p], pair_recv.at[p], partner)

    def finish_gram(p):
        p1, p2, p3 = acc[0], acc[1], acc[2]
        for ri, part in enumerate((p1 + p2, p3 - p1 + p2)):
            ebuf[ri, 0] = part[:, :128]
            ebuf[ri, 1] = part[:, 128:]
        for r in range(RANKS):
            for ri in range(2):
                for h in range(2):
                    lanes = pl.ds(h * 128, 128)
                    stage[p, r // PLANE, r % PLANE, ri, :, lanes] = ebuf[ri, h, pl.ds(r, 8, stride=32), :]
        go(pair_copy(p))

    def plane_stage(p):
        pair_copy(p).wait_recv()
        stage[p, core] += pair_in[p]

        def send(j, _):
            q = (place + j) % PLANE
            remote(
                stage.at[p, core, q], plane_in.at[p, place], plane_send.at[p], plane_recv.at[p],
                at_plane(core * PLANE + q),
            ).start()
            return 0

        lax.fori_loop(1, PLANE, send, 0)
        plane_in[p, place] = stage[p, core, place]

    def line_stage(p):
        waits(plane_in.at[p, pl.ds(0, PLANE - 1)], plane_recv.at[p])
        total = plane_in[p, 0]
        for q in range(1, PLANE):
            total = total + plane_in[p, q]
        line_in[p, z] = total

        def send(j, _):
            ref = line_in.at[p, z]
            remote(ref, ref, line_send.at[p], line_recv.at[p], at_z((z + j) % NZ)).start()
            return 0

        lax.fori_loop(1, NZ, send, 0)

    def full_stage(p):
        waits(line_in.at[p, pl.ds(0, NZ - 1)], line_recv.at[p])
        total = line_in[p, 0]
        for q in range(1, NZ):
            total = total + line_in[p, q]
        for ri in range(2):
            full[p * 8 : p * 8 + 8, ri, :] = total[ri]

    def pick_stage():
        def fill(d):
            sp, tl = at_plane(d)
            yy, cc = tl // 2, tl % 2
            for k, g in enumerate((sp * (2 * NY) + tl, sp * (2 * NY) + (yy + 1 - 2 * (yy % 2)) * 2 + cc)):
                for m in range(2):
                    first = k * 4 + m * 2
                    value = full[graphs[m, g]]
                    for h in range(2):
                        pick[d, h, first : first + 2, :] = value[:, h * 128 : h * 128 + 128]

        def send(j, _):
            d = (rank + j) % RANKS
            fill(d)
            remote(pick.at[d], picked.at[:, pl.ds(pl.multiple_of(rank * 8, 8), 8)], pick_send.at[0], pick_recv.at[0], at_plane(d)).start()
            return 0

        lax.fori_loop(1, RANKS, send, 0)
        fill(rank)
        for h in range(2):
            picked[h, pl.ds(pl.multiple_of(rank * 8, 8), 8), :] = pick[rank, h]

    def rows_stage():
        def send_rows(j, _):
            d = (rank + j) % RANKS
            _, tl = at_plane(d)
            rows[d, 0:2, :] = full[tl]
            rows[d, 2:4, :] = full[8 + tl]
            remote(rows.at[d], rowed.at[rank], rows_send.at[0], rows_recv.at[0], at_plane(d)).start()
            return 0

        lax.fori_loop(1, RANKS, send_rows, 0)
        rowed[rank, 0:2, :] = full[tile]
        rowed[rank, 2:4, :] = full[8 + tile]

    def convert(a):
        for s in range(NSPACE):
            for ri in range(2):
                hi, lo = split(tau[a, s, ri])
                tau_hi[a, ri, s * KDEV : (s + 1) * KDEV, :] = hi
                tau_lo[a, ri, s * KDEV : (s + 1) * KDEV, :] = lo

    norm = 1.0 / (NC * sites * NSPACE * 2 * NY)

    def moves(first_group):
        row = lax.broadcasted_iota(jnp.int32, (2 * BLOCK, 2 * BLOCK), 0)
        col = lax.broadcasted_iota(jnp.int32, (2 * BLOCK, 2 * BLOCK), 1)
        ri, a, i = row >> 7, row & 3, (row >> 2) & 31
        want = ri * BLOCK + ((a + first_group + ri) & 3) * 32 + i
        return (col == want).astype(F32).astype(BF16)

    def final():
        waits(picked.at[:, pl.ds(0, 8 * RANKS - 8)], pick_recv.at[0])
        pieces = []
        for k in range(2):
            u_re, u_im, v_re, v_im = (
                jnp.concatenate([picked[h, pl.ds(4 * k + m, RANKS, stride=8), :] for h in range(2)], axis=1)
                for m in range(4)
            )
            by_re = [split(v) for v in (u_re, u_im, v_re, v_im)]
            by_im = [split(v) for v in (-u_im, u_re, -v_im, v_re)]
            pieces.append((by_re, by_im))

        def weights(ri, part, a):
            return jnp.concatenate(
                [pieces[k][ri][(j - a) % 4][part] for k in range(2) for j in range(4)], axis=0
            )

        lane = lax.broadcasted_iota(jnp.int32, (1, 2 * BLOCK), 1)
        place_of = (lane >> 5) & 3
        groups = [None] * 4
        for a in range(SPIN):
            total = None
            for ri in range(2):
                w_hi, w_lo = weights(ri, 0, a), weights(ri, 1, a)
                hi, lo = tau_hi[a, ri], tau_lo[a, ri]
                new = dot(hi, w_hi) + dot(hi, w_lo) + dot(lo, w_hi)
                total = new if total is None else total + new
            for g in range(4):
                if groups[g] is None:
                    groups[g] = total
                else:
                    groups[g] = jnp.where(place_of == (a + g) % 4, total, groups[g])
        row_moves, col_moves = moves(0), moves(2)
        scale = norm / (NEV * math.sqrt(SPIN * NEV))
        nn = (((1,), (0,)), ((), ()))
        for k in (1, 0):
            lanes = slice(k * BLOCK, (k + 1) * BLOCK)
            uh, ul = split(jnp.concatenate([groups[0][:, lanes], groups[1][:, lanes]], axis=1))
            vh, vl = split(jnp.concatenate([groups[2][:, lanes], groups[3][:, lanes]], axis=1))
            c4 = dot(uh, vh, TN) + dot(uh, vl, TN) + dot(ul, vh, TN)
            hi, lo = split(c4 * scale)
            hi, lo = split(dot(row_moves, hi, nn) + dot(row_moves, lo, nn))
            c4 = dot(hi, col_moves) + dot(lo, col_moves)
            target = foreign if k == 1 else own_ref
            target[0] = c4[:BLOCK, :BLOCK] - c4[BLOCK:, BLOCK:]
            target[1] = c4[:BLOCK, BLOCK:] + c4[BLOCK:, :BLOCK]
            if k == 1:
                go(swap)

    mate = (space, (y + 1 - 2 * (y % 2)) * 2 + core)
    swap = remote(foreign, other_out, swap_send.at[0], swap_recv.at[0], mate)

    def elementals():
        waits(rowed.at[pl.ds(0, RANKS - 1)], rows_recv.at[0])
        width8 = NEV // NSPACE
        col = lax.broadcasted_iota(jnp.int32, (width8, NEV), 0)
        lane = lax.broadcasted_iota(jnp.int32, (width8, NEV), 1)
        ones = (lane == space * width8 + col).astype(F32)
        for k in range(4):
            el_ref[k // 2, k % 2] = lax.dot_general(
                ones, rowed[:, k, :], NT, precision=lax.Precision.HIGHEST, preferred_element_type=F32
            )

    small[0].wait()
    phases()
    small[1].wait()
    spread()
    small[2].wait()
    loads[0].wait()
    gram(0, 0)
    pl.semaphore_wait(barrier, RANKS - 1 + NZ - 1)
    tau_first()
    gram(0, 1)
    loads[1].wait()
    gram(0, 2)
    gram(0, 3)
    b_along_x(z, 0)
    loads[2].wait()
    gram(0, 4)
    b_z(1)
    a_z(0)
    gram(0, 5)
    finish_gram(0)
    gram(1, 0)
    b_z(2)
    gram(1, 1)
    plane_stage(0)
    gram(1, 2)
    b_push(0)
    b_z(3)
    gram(1, 3)
    a_z(1)
    gram(1, 4)
    b_push(1)
    b_push(5)
    gram(1, 5)
    finish_gram(1)
    b_z(4)
    plane_stage(1)
    a_z(2)
    b_push(2)
    b_push(6)
    line_stage(0)
    b_push(3)
    b_push(7)
    b_push(4)
    a_z(3)
    line_stage(1)
    a_z(4)
    full_stage(0)
    for k in range(2 * NZ):
        waits(tau.at[0, pl.ds(0, NX)], push_recv.at[k])
    for a in range(SPIN):
        convert(a)
    full_stage(1)
    pick_stage()
    rows_stage()
    final()
    own_copy = pltpu.make_async_copy(own_ref, own_out, out_sem.at[0])
    own_copy.start()
    elementals()
    el_copy = pltpu.make_async_copy(el_ref, el_out, out_sem.at[1])
    el_copy.start()
    swap.wait_recv()
    own_copy.wait()
    el_copy.wait()
    for copy in started:
        copy.wait_send()
    for p in range(NMOM):
        waits(plane_in.at[p, pl.ds(0, PLANE - 1)], plane_send.at[p])
        waits(line_in.at[p, pl.ds(0, NZ - 1)], line_send.at[p])
    waits(picked.at[:, pl.ds(0, 8 * RANKS - 8)], pick_send.at[0])
    waits(rowed.at[pl.ds(0, RANKS - 1)], rows_send.at[0])


def per_device(eigenvectors, perambulator, momenta, graph_blocks):
    sites = eigenvectors.shape[3]
    eig = eigenvectors.transpose(0, 2, 1, 3)
    dma = pltpu.SemaphoreType.DMA
    width8 = NEV // NSPACE
    el, own, other = pl.pallas_call(
        kernel,
        out_shape=(
            jax.ShapeDtypeStruct((NMOM, 2, width8, 32), F32),
            jax.ShapeDtypeStruct((2, BLOCK, BLOCK), F32),
            jax.ShapeDtypeStruct((2, BLOCK, BLOCK), F32),
        ),
        in_specs=[
            pl.BlockSpec(memory_space=pl.ANY),
            pl.BlockSpec(memory_space=pl.ANY),
            pl.BlockSpec(memory_space=pl.ANY),
            pl.BlockSpec(memory_space=pl.ANY),
        ],
        out_specs=(pl.BlockSpec(memory_space=pl.ANY),) * 3,
        scratch_shapes=[
            pltpu.SMEM((NMOM, 3), jnp.int32),
            pltpu.SMEM((2, NSPACE * 2 * NY), jnp.int32),
            pltpu.VMEM((2, 2 * KDEV, SPIN * NEV), F32),
            pltpu.VMEM((NMOM, 2, width8, 32), F32),
            pltpu.VMEM((2, BLOCK, BLOCK), F32),
            pltpu.VMEM((2, NC, NEV, sites), F32),
            pltpu.VMEM((3, NC, 2 * NEV, sites), BF16),
            pltpu.VMEM((NMOM, 2, sites), F32),
            pltpu.VMEM((3, NEV, NEV), F32),
            pltpu.VMEM((2, 2, NEV, 128), F32),
            pltpu.VMEM((NMOM, 2, PLANE, 2, 8, NEV), F32),
            pltpu.VMEM((NMOM, PLANE, 2, 8, NEV), F32),
            pltpu.VMEM((NMOM, PLANE, 2, 8, NEV), F32),
            pltpu.VMEM((NMOM, NZ, 2, 8, NEV), F32),
            pltpu.VMEM((16, 2, NEV), F32),
            pltpu.VMEM((RANKS, 2, 8, 128), F32),
            pltpu.VMEM((2, RANKS * 8, 128), F32),
            pltpu.VMEM((RANKS, 4, NEV), F32),
            pltpu.VMEM((RANKS, 4, NEV), F32),
            pltpu.VMEM((SPIN, 2, KDEV, NEV), F32),
            pltpu.VMEM((SPIN, NSPACE, 2, KDEV, NEV), F32),
            pltpu.VMEM((SPIN, 2, NSPACE * KDEV, NEV), BF16),
            pltpu.VMEM((SPIN, 2, NSPACE * KDEV, NEV), BF16),
            pltpu.VMEM((2, BLOCK, BLOCK), F32),
            dma((NC,)),
            dma((2,)),
            dma((NMOM,)),
            dma((NMOM,)),
            dma((NMOM,)),
            dma((NMOM,)),
            dma((NMOM,)),
            dma((NMOM,)),
            dma((1,)),
            dma((1,)),
            dma((1,)),
            dma((1,)),
            dma((NX - 1,)),
            dma((1,)),
            dma((2, NZ // 2)),
            dma((2, NZ // 2)),
            dma((2, NZ // 2)),
            dma((2, NZ // 2)),
            dma((NZ, NX - 1)),
            dma((NZ,)),
            dma((2 * NZ,)),
            dma((2 * NZ,)),
            dma((1,)),
            dma((1,)),
            dma((3,)),
            dma((2,)),
        ],
        compiler_params=pltpu.CompilerParams(
            collective_id=0, has_side_effects=True, vmem_limit_bytes=60 * 2**20
        ),
    )(momenta, graph_blocks.T, eig, perambulator)
    norm = 1.0 / math.sqrt(NC * sites * NSPACE * 2 * NY)

    def finish(el_ref, own_ref, other_ref, el_out, sum_out):
        el_out[...] = el_ref[...] * norm
        sum_out[...] = own_ref[...] + other_ref[...]

    el, out = pl.pallas_call(
        finish,
        out_shape=(jax.ShapeDtypeStruct(el.shape, F32), jax.ShapeDtypeStruct(own.shape, F32)),
    )(el, own, other)
    return el.transpose(0, 1, 3, 2), out[None]


def solution(mesh):
    return jax.shard_map(
        per_device,
        mesh=mesh,
        in_specs=(P(None, None, None, ("space", "tile")), P(None, "space", None), P(), P()),
        out_specs=(P(None, None, "tile", "space"), P(("space", "tile"), None, None, None)),
        check_vma=False,
    )
```

time: 81.4 us -> 61.2 us (0.75)
  Pallas kernels: 73.6 us -> 59.6 us
  local copies, waits for them, and re-layouts: 6.88 us -> 0 us
    pallas_call x1 -> x2, Pallas kernels: 73.6 us -> 59.6 us  [the longest x1 57.9 us: per_device(): pl.pallas_call(kernel, out_shape=(jax.ShapeDtypeStruct((NMOM, 2, width8,...]
    unnamed x4 -> x0, local copies, waits for them, and re-layouts: 5.84 us -> none
    reshape x1 -> x0, local copies, waits for them, and re-layouts: 1.04 us -> none  [per_device(): tau_in = perambulator.reshape(2, -1, NEV, SPIN).transpose(3, 0, 1, 2)]
where the time goes in v2:
time: 61.2 us; the launch traced here: 60.2 us
  Pallas kernels  59.6 us (97%)
  between operations  0.64 us (1%)
    pallas_call x1, Pallas kernels, per_device(): pl.pallas_call(kernel, out_shape=(jax.ShapeDtypeStruct((NMOM, 2, width8,...  57.9 us
    pallas_call x1, Pallas kernels, per_device(): pl.pallas_call(finish, out_shape=(jax.ShapeDtypeStruct(el.shape, F32), ja...  1.66 us

profile of v2, /device:TPU:1, one launch (start us, length us, event | category | flops | bytes accessed | tf_op | source)
XLA Modules:
  0.0 60.2 jit_solution(12747526304797156623)
XLA Ops:
  0.6 57.9 %shard_map.59 = (f32[2,2,8,32]{3,2,1,0:T(8,128)}, f32[2,128,128]{2,1,0:T(8,128)}, f32[2,128,128]{2,1,0:T(8,128)}) custom-call(s32[2,3]{1,0:T(2,128)} %momenta_in.1, s32[2,256]{1,0:T(2,128)} %bitcast.5, f32[2,3,256,1024]{3,2,1,0:T(8,128)} %bitcast.4, f32[2,32,1024]{2,1,0:T(8,128)} %sources_in.1), custom_call_target="tpu_custom_call" | custom-call | tf_op jit(solution)/shard_map/pallas_call | solution.py:484
  58.6 1.7 %shard_map.60 = (f32[2,2,8,32]{3,2,1,0:T(8,128)}, f32[2,128,128]{2,1,0:T(8,128)}) custom-call(f32[2,2,8,32]{3,2,1,0:T(8,128)} %get-tuple-element.7.el_ref, f32[2,128,128]{2,1,0:T(8,128)} %get-tuple-element.8.own_ref, f32[2,128,128]{2,1,0:T(8,128)} %get-tuple-element.9.other_ref), custom_call_target="tpu_custom_call" | custom-call | tf_op jit(solution)/shard_map/pallas_call | solution.py:560

commit v3 on v2

--- a/solution.py
+++ b/solution.py
@@ -20,6 +20,12 @@
 BLOCK = 128
 KDEV = 16
 MESH = pl.DeviceIdType.MESH
+PLANE_FAR = tuple(
+    sorted(
+        ((dx, dy) for dx in range(NX) for dy in range(NY) if dx or dy),
+        key=lambda d: -min(d[0], NX - d[0]) - min(d[1], NY - d[1]),
+    )
+)
 F32 = jnp.float32
 BF16 = jnp.bfloat16
 NT = (((1,), (1,)), ((), ()))
@@ -38,7 +44,7 @@
 def kernel(
     momenta_in, graphs_in, eig, sources_in, el_out, own_out, other_out,
     momenta, graphs, sources, el_ref, own_ref, vec, left, trig, acc, ebuf, stage, pair_in, plane_in, line_in, full, pick, picked, rows, rowed,
-    tau_in, tau, tau_hi, tau_lo, foreign,
+    tau_in, tau, tau_hi, tau_lo, wts, foreign,
     load_sem, own_sem, pair_send, pair_recv, plane_send, plane_recv, line_send, line_recv,
     pick_send, pick_recv, rows_send, rows_recv,
     ax_send, ax_recv, az_send, az_recv, bz_send, bz_recv, bx_send, bx_recv, push_send, push_recv, swap_send, swap_recv, small_sem, out_sem,
@@ -123,11 +129,8 @@
                         ri * KDEV : (ri + 1) * KDEV, a * 128 : a * 128 + 128
                     ]
 
-    started = []
-
     def go(copy):
         copy.start()
-        started.append(copy)
 
     def bundle(a, zz):
         return tau.at[a, pl.ds(zz * NX, NX)]
@@ -136,7 +139,7 @@
         return tau.at[a, pl.ds(zz * NX + h * (NX // 2), NX // 2)]
 
     def push(a, zz, k):
-        go(remote(bundle(a, zz), bundle(a, zz), push_send.at[k], push_recv.at[k], partner))
+        go(remote(bundle(a, zz), bundle(a, zz), push_send.at[0], push_recv.at[0], partner))
 
     def waits(ref, sem):
         pltpu.make_async_copy(ref, ref, sem).wait()
@@ -144,7 +147,7 @@
     def b_along_x(zz, k):
         for j in range(1, NX):
             ref = tau.at[a_b, zz * NX + x]
-            go(remote(ref, ref, bx_send.at[k, j - 1], bx_recv.at[k], at_x((x + j) % NX)))
+            go(remote(ref, ref, bx_send.at[0], bx_recv.at[k], at_x((x + j) % NX)))
 
     def z_back(h):
         return (z + NZ - h) % NZ
@@ -163,10 +166,10 @@
             copy.wait()
         for j in range(1, NX):
             ref = tau.at[a_a, slot]
-            go(remote(ref, ref, ax_send.at[j - 1], ax_recv.at[0], at_x((x + j) % NX)))
+            go(remote(ref, ref, ax_send.at[0], ax_recv.at[0], at_x((x + j) % NX)))
         ref = tau.at[a_b, slot]
-        go(remote(ref, ref, bz_send.at[0, 0], bz_recv.at[0, 0], at_z(z_on(1))))
-        go(remote(ref, ref, bz_send.at[1, 0], bz_recv.at[1, 0], at_z(z_back(1))))
+        go(remote(ref, ref, bz_send.at[0], bz_recv.at[0, 0], at_z(z_on(1))))
+        go(remote(ref, ref, bz_send.at[0], bz_recv.at[1, 0], at_z(z_back(1))))
 
     def b_z(h):
         up, down = z_back(h), z_on(h)
@@ -178,8 +181,8 @@
                 ref_u, ref_d = ref_up.at[0], ref_down.at[1]
             else:
                 ref_u, ref_d = ref_up, ref_down
-            go(remote(ref_u, ref_u, bz_send.at[0, h], bz_recv.at[0, h], at_z(z_on(1))))
-            go(remote(ref_d, ref_d, bz_send.at[1, h], bz_recv.at[1, h], at_z(z_back(1))))
+            go(remote(ref_u, ref_u, bz_send.at[0], bz_recv.at[0, h], at_z(z_on(1))))
+            go(remote(ref_d, ref_d, bz_send.at[0], bz_recv.at[1, h], at_z(z_back(1))))
             b_along_x(up, h)
             b_along_x(down, NZ // 2 + h)
         else:
@@ -192,51 +195,57 @@
         waits(tau.at[a_b, pl.ds(0, NX - 1)], bx_recv.at[k])
         push(a_b, zz, NZ + k)
 
-    def a_z(h):
+    def a_z(h, part):
         up, down = z_back(h), z_on(h)
+
+        def onward(ref, way):
+            to = at_z(z_on(1)) if way == 0 else at_z(z_back(1))
+            go(remote(ref, ref, az_send.at[0], az_recv.at[way, h, part], to))
+
+        def push_half(zz, k):
+            ref = half_bundle(a_a, zz, part)
+            go(remote(ref, ref, push_send.at[0], push_recv.at[0], partner))
+
         if h == 0:
-            waits(tau.at[a_a, pl.ds(0, NX - 1)], ax_recv.at[0])
-            go(remote(bundle(a_a, z), bundle(a_a, z), az_send.at[0, 0], az_recv.at[0, 0], at_z(z_on(1))))
-            go(remote(bundle(a_a, z), bundle(a_a, z), az_send.at[1, 0], az_recv.at[1, 0], at_z(z_back(1))))
-            push(a_a, z, 0)
+            if part == 0:
+                waits(tau.at[a_a, pl.ds(0, NX - 1)], ax_recv.at[0])
+            onward(half_bundle(a_a, z, part), 0)
+            onward(half_bundle(a_a, z, part), 1)
+            push_half(z, 0)
         elif h < NZ // 2:
-            waits(bundle(a_a, up), az_recv.at[0, h - 1])
-            waits(bundle(a_a, down), az_recv.at[1, h - 1])
-            if h + 1 == NZ // 2:
-                ref_u, ref_d = half_bundle(a_a, up, 0), half_bundle(a_a, down, 1)
-            else:
-                ref_u, ref_d = bundle(a_a, up), bundle(a_a, down)
-            go(remote(ref_u, ref_u, az_send.at[0, h], az_recv.at[0, h], at_z(z_on(1))))
-            go(remote(ref_d, ref_d, az_send.at[1, h], az_recv.at[1, h], at_z(z_back(1))))
-            push(a_a, up, h)
-            push(a_a, down, NZ // 2 + h)
+            waits(half_bundle(a_a, up, part), az_recv.at[0, h - 1, part])
+            waits(half_bundle(a_a, down, part), az_recv.at[1, h - 1, part])
+            if h + 1 < NZ // 2 or part == 0:
+                onward(half_bundle(a_a, up, part), 0)
+            if h + 1 < NZ // 2 or part == 1:
+                onward(half_bundle(a_a, down, part), 1)
+            push_half(up, h)
+            push_half(down, NZ // 2 + h)
         else:
-            waits(half_bundle(a_a, up, 0), az_recv.at[0, h - 1])
-            waits(half_bundle(a_a, up, 1), az_recv.at[1, h - 1])
-            push(a_a, up, h)
-
-    width = 512
-
-    def gram(p, step):
-        c, b = step // 2, step % 2
-        cols = slice(b * width, (b + 1) * width)
-        r, i = vec[0, c, :, cols], vec[1, c, :, cols]
-        co, si = trig[p, 0:1, cols], trig[p, 1:2, cols]
-        wr = co * r + si * i
-        wi = co * i - si * r
-        for k, (lhs, rhs) in enumerate(((r, wr), (i, wi), (None, wr + wi))):
-            if p == 0:
-                lh, ll = split(r - i if lhs is None else lhs)
-                left[k, c, :NEV, cols] = lh
-                left[k, c, NEV:, cols] = ll
-            else:
-                lh, ll = left[k, c, :NEV, cols], left[k, c, NEV:, cols]
-            rh, rl = split(rhs)
-            new = dot(lh, rh) + dot(lh, rl) + dot(ll, rh)
-            if step == 0:
-                acc[k] = new
-            else:
-                acc[k] += new
+            waits(half_bundle(a_a, up, part), az_recv.at[part, h - 1, part])
+            push_half(up, h)
+
+    zero = space // NSPACE
+
+    def gram(p, c):
+        def body(c, _):
+            r, i = vec[0, c], vec[1, c]
+            co, si = trig[p, 0:1, :], trig[p, 1:2, :]
+            wr = co * r + si * i
+            wi = co * i - si * r
+            for k, (lhs, rhs) in enumerate(((r, wr), (i, wi), (None, wr + wi))):
+                if p == 0:
+                    lh, ll = split(r - i if lhs is None else lhs)
+                    left[k, c, :NEV] = lh
+                    left[k, c, NEV:] = ll
+                else:
+                    lh, ll = left[k, c, :NEV], left[k, c, NEV:]
+                rh, rl = split(rhs)
+                wide = dot(jnp.concatenate([lh, ll], axis=0), rh)
+                acc[k] += wide[:NEV] + wide[NEV:] + dot(lh, rl)
+            return 0
+
+        lax.fori_loop(zero + c, zero + c + 1, body, 0)
 
     def pair_copy(p):
         return remote(stage.at[p, 1 - core], pair_in.at[p], pair_send.at[p], pair_recv.at[p], partner)
@@ -257,15 +266,12 @@
         pair_copy(p).wait_recv()
         stage[p, core] += pair_in[p]
 
-        def send(j, _):
-            q = (place + j) % PLANE
+        for dx, dy in PLANE_FAR:
+            q = ((x + dx) % NX) * NY + (y + dy) % NY
             remote(
                 stage.at[p, core, q], plane_in.at[p, place], plane_send.at[p], plane_recv.at[p],
                 at_plane(core * PLANE + q),
             ).start()
-            return 0
-
-        lax.fori_loop(1, PLANE, send, 0)
         plane_in[p, place] = stage[p, core, place]
 
     def line_stage(p):
@@ -275,12 +281,9 @@
             total = total + plane_in[p, q]
         line_in[p, z] = total
 
-        def send(j, _):
+        for dz in (4, 3, 5, 2, 6, 1, 7):
             ref = line_in.at[p, z]
-            remote(ref, ref, line_send.at[p], line_recv.at[p], at_z((z + j) % NZ)).start()
-            return 0
-
-        lax.fori_loop(1, NZ, send, 0)
+            remote(ref, ref, line_send.at[p], line_recv.at[p], at_z((z + dz) % NZ)).start()
 
     def full_stage(p):
         waits(line_in.at[p, pl.ds(0, NZ - 1)], line_recv.at[p])
@@ -301,13 +304,14 @@
                     for h in range(2):
                         pick[d, h, first : first + 2, :] = value[:, h * 128 : h * 128 + 128]
 
-        def send(j, _):
-            d = (rank + j) % RANKS
-            fill(d)
-            remote(pick.at[d], picked.at[:, pl.ds(pl.multiple_of(rank * 8, 8), 8)], pick_send.at[0], pick_recv.at[0], at_plane(d)).start()
-            return 0
-
-        lax.fori_loop(1, RANKS, send, 0)
+        for dx, dy in PLANE_FAR + ((0, 0),):
+            for cc in (core, 1 - core):
+                if (dx, dy) == (0, 0) and cc is core:
+                    continue
+                d = cc * PLANE + ((x + dx) % NX) * NY + (y + dy) % NY
+                fill(d)
+                remote(pick.at[d], picked.at[:, pl.ds(pl.multiple_of(rank * 8, 8), 8)], pick_send.at[0], pick_recv.at[0], at_plane(d)).start()
+
         fill(rank)
         for h in range(2):
             picked[h, pl.ds(pl.multiple_of(rank * 8, 8), 8), :] = pick[rank, h]
@@ -343,43 +347,41 @@
 
     def final():
         waits(picked.at[:, pl.ds(0, 8 * RANKS - 8)], pick_recv.at[0])
-        pieces = []
         for k in range(2):
             u_re, u_im, v_re, v_im = (
                 jnp.concatenate([picked[h, pl.ds(4 * k + m, RANKS, stride=8), :] for h in range(2)], axis=1)
                 for m in range(4)
             )
-            by_re = [split(v) for v in (u_re, u_im, v_re, v_im)]
-            by_im = [split(v) for v in (-u_im, u_re, -v_im, v_re)]
-            pieces.append((by_re, by_im))
-
-        def weights(ri, part, a):
-            return jnp.concatenate(
-                [pieces[k][ri][(j - a) % 4][part] for k in range(2) for j in range(4)], axis=0
-            )
-
-        lane = lax.broadcasted_iota(jnp.int32, (1, 2 * BLOCK), 1)
-        place_of = (lane >> 5) & 3
-        groups = [None] * 4
-        for a in range(SPIN):
-            total = None
-            for ri in range(2):
-                w_hi, w_lo = weights(ri, 0, a), weights(ri, 1, a)
-                hi, lo = tau_hi[a, ri], tau_lo[a, ri]
-                new = dot(hi, w_hi) + dot(hi, w_lo) + dot(lo, w_hi)
-                total = new if total is None else total + new
-            for g in range(4):
-                if groups[g] is None:
-                    groups[g] = total
-                else:
-                    groups[g] = jnp.where(place_of == (a + g) % 4, total, groups[g])
+            for ri, values in enumerate(((u_re, u_im, v_re, v_im), (-u_im, u_re, -v_im, v_re))):
+                for j, value in enumerate(values):
+                    for part, half in enumerate(split(value)):
+                        wts[ri, part, k, j * 32 : j * 32 + 32, :] = half
+                        if j < 3:
+                            wts[ri, part, k, j * 32 + BLOCK : j * 32 + BLOCK + 32, :] = half
+
+        lane = lax.broadcasted_iota(jnp.int32, (1, BLOCK), 1)
+        place_of = lane >> 5
         row_moves, col_moves = moves(0), moves(2)
         scale = norm / (NEV * math.sqrt(SPIN * NEV))
         nn = (((1,), (0,)), ((), ()))
         for k in (1, 0):
-            lanes = slice(k * BLOCK, (k + 1) * BLOCK)
-            uh, ul = split(jnp.concatenate([groups[0][:, lanes], groups[1][:, lanes]], axis=1))
-            vh, vl = split(jnp.concatenate([groups[2][:, lanes], groups[3][:, lanes]], axis=1))
+            groups = [None] * 4
+            for a in range(SPIN):
+                first = (-a % 4) * 32
+                total = None
+                for ri in range(2):
+                    w_hi = wts[ri, 0, k, first : first + BLOCK, :]
+                    both = jnp.concatenate([w_hi, wts[ri, 1, k, first : first + BLOCK, :]], axis=0)
+                    wide = dot(tau_hi[a, ri], both)
+                    new = wide[:, :BLOCK] + wide[:, BLOCK:] + dot(tau_lo[a, ri], w_hi)
+                    total = new if total is None else total + new
+                for g in range(4):
+                    if groups[g] is None:
+                        groups[g] = total
+                    else:
+                        groups[g] = jnp.where(place_of == (a + g) % 4, total, groups[g])
+            uh, ul = split(jnp.concatenate([groups[0], groups[1]], axis=1))
+            vh, vl = split(jnp.concatenate([groups[2], groups[3]], axis=1))
             c4 = dot(uh, vh, TN) + dot(uh, vl, TN) + dot(ul, vh, TN)
             hi, lo = split(c4 * scale)
             hi, lo = split(dot(row_moves, hi, nn) + dot(row_moves, lo, nn))
@@ -404,60 +406,60 @@
                 ones, rowed[:, k, :], NT, precision=lax.Precision.HIGHEST, preferred_element_type=F32
             )
 
+    acc[...] = jnp.zeros_like(acc)
     small[0].wait()
     phases()
+    loads[0].wait()
+    gram(0, 0)
     small[1].wait()
     spread()
     small[2].wait()
-    loads[0].wait()
-    gram(0, 0)
     pl.semaphore_wait(barrier, RANKS - 1 + NZ - 1)
     tau_first()
+    loads[1].wait()
     gram(0, 1)
-    loads[1].wait()
-    gram(0, 2)
-    gram(0, 3)
     b_along_x(z, 0)
     loads[2].wait()
-    gram(0, 4)
+    gram(0, 2)
+    finish_gram(0)
+    acc[...] = jnp.zeros_like(acc)
     b_z(1)
-    a_z(0)
-    gram(0, 5)
-    finish_gram(0)
+    a_z(0, 0)
+    a_z(0, 1)
     gram(1, 0)
+    plane_stage(0)
+    gram(1, 1)
     b_z(2)
-    gram(1, 1)
-    plane_stage(0)
+    a_z(1, 0)
+    b_push(0)
     gram(1, 2)
-    b_push(0)
+    finish_gram(1)
+    a_z(1, 1)
+    plane_stage(1)
     b_z(3)
-    gram(1, 3)
-    a_z(1)
-    gram(1, 4)
+    a_z(2, 0)
     b_push(1)
     b_push(5)
-    gram(1, 5)
-    finish_gram(1)
+    line_stage(0)
+    a_z(2, 1)
     b_z(4)
-    plane_stage(1)
-    a_z(2)
+    a_z(3, 0)
     b_push(2)
     b_push(6)
-    line_stage(0)
+    line_stage(1)
+    a_z(3, 1)
     b_push(3)
     b_push(7)
     b_push(4)
-    a_z(3)
-    line_stage(1)
-    a_z(4)
     full_stage(0)
-    for k in range(2 * NZ):
-        waits(tau.at[0, pl.ds(0, NX)], push_recv.at[k])
+    a_z(4, 0)
+    full_stage(1)
+    pick_stage()
+    a_z(4, 1)
+    rows_stage()
+    waits(tau.at[pl.ds(0, 2)], push_recv.at[0])
     for a in range(SPIN):
         convert(a)
-    full_stage(1)
-    pick_stage()
-    rows_stage()
     final()
     own_copy = pltpu.make_async_copy(own_ref, own_out, out_sem.at[0])
     own_copy.start()
@@ -467,9 +469,14 @@
     swap.wait_recv()
     own_copy.wait()
     el_copy.wait()
-    for copy in started:
-        copy.wait_send()
+    waits(tau.at[0, pl.ds(0, NX - 1)], ax_send.at[0])
+    waits(tau.at[0, pl.ds(0, NX * (NZ - 1))], az_send.at[0])
+    waits(tau.at[0, pl.ds(0, NZ - 1)], bz_send.at[0])
+    waits(tau.at[0, pl.ds(0, NZ * (NX - 1))], bx_send.at[0])
+    waits(tau.at[pl.ds(0, 2)], push_send.at[0])
+    swap.wait_send()
     for p in range(NMOM):
+        pair_copy(p).wait_send()
         waits(plane_in.at[p, pl.ds(0, PLANE - 1)], plane_send.at[p])
         waits(line_in.at[p, pl.ds(0, NZ - 1)], line_send.at[p])
     waits(picked.at[:, pl.ds(0, 8 * RANKS - 8)], pick_send.at[0])
@@ -489,10 +496,10 @@
             jax.ShapeDtypeStruct((2, BLOCK, BLOCK), F32),
         ),
         in_specs=[
-            pl.BlockSpec(memory_space=pl.ANY),
-            pl.BlockSpec(memory_space=pl.ANY),
-            pl.BlockSpec(memory_space=pl.ANY),
-            pl.BlockSpec(memory_space=pl.ANY),
+            pl.BlockSpec(memory_space=pltpu.HBM),
+            pl.BlockSpec(memory_space=pltpu.HBM),
+            pl.BlockSpec(memory_space=pltpu.HBM),
+            pl.BlockSpec(memory_space=pltpu.HBM),
         ],
         out_specs=(pl.BlockSpec(memory_space=pl.ANY),) * 3,
         scratch_shapes=[
@@ -519,6 +526,7 @@
             pltpu.VMEM((SPIN, NSPACE, 2, KDEV, NEV), F32),
             pltpu.VMEM((SPIN, 2, NSPACE * KDEV, NEV), BF16),
             pltpu.VMEM((SPIN, 2, NSPACE * KDEV, NEV), BF16),
+            pltpu.VMEM((2, 2, 2, 7 * 32, NEV), BF16),
             pltpu.VMEM((2, BLOCK, BLOCK), F32),
             dma((NC,)),
             dma((2,)),
@@ -532,34 +540,58 @@
             dma((1,)),
             dma((1,)),
             dma((1,)),
-            dma((NX - 1,)),
+            dma((1,)),
+            dma((1,)),
+            dma((1,)),
+            dma((2, NZ // 2, 2)),
             dma((1,)),
             dma((2, NZ // 2)),
-            dma((2, NZ // 2)),
-            dma((2, NZ // 2)),
-            dma((2, NZ // 2)),
-            dma((NZ, NX - 1)),
+            dma((1,)),
             dma((NZ,)),
-            dma((2 * NZ,)),
-            dma((2 * NZ,)),
+            dma((1,)),
+            dma((1,)),
             dma((1,)),
             dma((1,)),
             dma((3,)),
             dma((2,)),
         ],
         compiler_params=pltpu.CompilerParams(
-            collective_id=0, has_side_effects=True, vmem_limit_bytes=60 * 2**20
+            collective_id=0, has_side_effects=True, vmem_limit_bytes=48 * 2**20
         ),
-    )(momenta, graph_blocks.T, eig, perambulator)
+    )(*(pltpu.with_memory_space_constraint(v, pltpu.HBM) for v in (momenta, graph_blocks.T, eig, perambulator)))
     norm = 1.0 / math.sqrt(NC * sites * NSPACE * 2 * NY)
 
-    def finish(el_ref, own_ref, other_ref, el_out, sum_out):
-        el_out[...] = el_ref[...] * norm
-        sum_out[...] = own_ref[...] + other_ref[...]
-
+    def finish(el_ref, own_ref, other_ref, el_out, sum_out, el_buf, own_buf, other_buf, sems):
+        pairs = ((own_ref, own_buf), (other_ref, other_buf), (el_ref, el_buf))
+        copies = [pltpu.make_async_copy(a, b, sems.at[k]) for k, (a, b) in enumerate(pairs)]
+        for copy in copies:
+            copy.start()
+        copies[0].wait()
+        copies[1].wait()
+        own_buf[...] += other_buf[...]
+        sum_copy = pltpu.make_async_copy(own_buf, sum_out, sems.at[3])
+        sum_copy.start()
+        copies[2].wait()
+        el_buf[...] *= norm
+        el_copy = pltpu.make_async_copy(el_buf, el_out, sems.at[4])
+        el_copy.start()
+        sum_copy.wait()
+        el_copy.wait()
+
+    anywhere = pl.BlockSpec(memory_space=pl.ANY)
+    hbm = pl.BlockSpec(memory_space=pltpu.HBM)
     el, out = pl.pallas_call(
         finish,
         out_shape=(jax.ShapeDtypeStruct(el.shape, F32), jax.ShapeDtypeStruct(own.shape, F32)),
+        in_specs=[anywhere] * 3,
+        out_specs=(hbm, hbm),
+        scratch_shapes=[
+            pltpu.VMEM(el.shape, F32),
+            pltpu.VMEM(own.shape, F32),
+            pltpu.VMEM(own.shape, F32),
+            dma((5,)),
+        ],
+        compiler_params=pltpu.CompilerParams(vmem_limit_bytes=8 * 2**20),
     )(el, own, other)
     return el.transpose(0, 1, 3, 2), out[None]
 

time: 61.2 us -> 52.1 us (0.85); the launches traced: 60.2 us -> 52 us
  Pallas kernels: 59.6 us -> 51.2 us
    pallas_call x1, Pallas kernels: 57.9 us -> 50.1 us  [per_device(): pl.pallas_call(kernel, out_shape=(jax.ShapeDtypeStruct((NMOM, 2, width8,...]
where the time goes in v3:
time: 52.1 us; the launch traced here: 52 us
  Pallas kernels  51.2 us (98%)
  between operations  0.8 us (2%)
    pallas_call x1, Pallas kernels, per_device(): pl.pallas_call(kernel, out_shape=(jax.ShapeDtypeStruct((NMOM, 2, width8,...  50.1 us
    pallas_call x1, Pallas kernels, per_device(): pl.pallas_call(finish, out_shape=(jax.ShapeDtypeStruct(el.shape, F32), ja...  1.08 us

profile of v3, /device:TPU:1, one launch (start us, length us, event | category | flops | bytes accessed | tf_op | source)
XLA Modules:
  0.0 52.0 jit_solution(14436877897668586499)
XLA Ops:
  0.6 50.1 %shard_map.59 = (f32[2,2,8,32]{3,2,1,0:T(8,128)S(1)}, f32[2,128,128]{2,1,0:T(8,128)S(1)}, f32[2,128,128]{2,1,0:T(8,128)S(1)}) custom-call(s32[2,3]{1,0:T(2,128)} %momenta_in.1, s32[2,256]{1,0:T(2,128)} %bitcast.5, f32[2,3,256,1024]{3,2,1,0:T(8,128)} %bitcast.4, f32[2,32,1024]{2,1,0:T(8,128)} %sources_in.1), custom_call_target="tpu_custom_call" | custom-call | tf_op jit(solution)/shard_map/pallas_call | solution.py:491
  50.7 1.1 %shard_map.60 = (f32[2,2,8,32]{3,2,1,0:T(8,128)}, f32[2,128,128]{2,1,0:T(8,128)}) custom-call(f32[2,2,8,32]{3,2,1,0:T(8,128)S(1)} %get-tuple-element.7.el_ref, f32[2,128,128]{2,1,0:T(8,128)S(1)} %get-tuple-element.8.own_ref, f32[2,128,128]{2,1,0:T(8,128)S(1)} %get-tuple-element.9.other_ref), custom_call_target="tpu_custom_call" | custom-call | tf_op jit(solution)/shard_map/pallas_call | solution.py:583

commit v4 on v3

--- a/solution.py
+++ b/solution.py
@@ -69,6 +69,9 @@
 
     partner = (space, y * 2 + 1 - core)
 
+    def mate_row(yy, c):
+        return (yy + NY + 1 - 2 * ((yy + c) % 2)) % NY
+
     def remote(src, dst, send, recv, device):
         return pltpu.make_async_remote_copy(
             src_ref=src, dst_ref=dst, send_sem=send, recv_sem=recv, device_id=device, device_id_type=MESH
@@ -293,28 +296,26 @@
         for ri in range(2):
             full[p * 8 : p * 8 + 8, ri, :] = total[ri]
 
-    def pick_stage():
+    def pick_stage(k):
         def fill(d):
             sp, tl = at_plane(d)
             yy, cc = tl // 2, tl % 2
-            for k, g in enumerate((sp * (2 * NY) + tl, sp * (2 * NY) + (yy + 1 - 2 * (yy % 2)) * 2 + cc)):
-                for m in range(2):
-                    first = k * 4 + m * 2
-                    value = full[graphs[m, g]]
-                    for h in range(2):
-                        pick[d, h, first : first + 2, :] = value[:, h * 128 : h * 128 + 128]
-
+            g = sp * (2 * NY) + (tl if k == 0 else mate_row(yy, cc) * 2 + cc)
+            for m in range(2):
+                value = full[graphs[m, g]]
+                for h in range(2):
+                    pick[k, d, h * 4 + m * 2 : h * 4 + m * 2 + 2, :] = value[:, h * 128 : h * 128 + 128]
+
+        here = picked.at[k, pl.ds(pl.multiple_of(rank * 8, 8), 8)]
         for dx, dy in PLANE_FAR + ((0, 0),):
             for cc in (core, 1 - core):
                 if (dx, dy) == (0, 0) and cc is core:
                     continue
                 d = cc * PLANE + ((x + dx) % NX) * NY + (y + dy) % NY
                 fill(d)
-                remote(pick.at[d], picked.at[:, pl.ds(pl.multiple_of(rank * 8, 8), 8)], pick_send.at[0], pick_recv.at[0], at_plane(d)).start()
-
+                remote(pick.at[k, d], here, pick_send.at[k], pick_recv.at[k], at_plane(d)).start()
         fill(rank)
-        for h in range(2):
-            picked[h, pl.ds(pl.multiple_of(rank * 8, 8), 8), :] = pick[rank, h]
+        picked[k, pl.ds(pl.multiple_of(rank * 8, 8), 8), :] = pick[k, rank]
 
     def rows_stage():
         def send_rows(j, _):
@@ -346,10 +347,10 @@
         return (col == want).astype(F32).astype(BF16)
 
     def final():
-        waits(picked.at[:, pl.ds(0, 8 * RANKS - 8)], pick_recv.at[0])
-        for k in range(2):
+        def weigh(k):
+            waits(picked.at[k, pl.ds(0, 8 * RANKS - 8)], pick_recv.at[k])
             u_re, u_im, v_re, v_im = (
-                jnp.concatenate([picked[h, pl.ds(4 * k + m, RANKS, stride=8), :] for h in range(2)], axis=1)
+                jnp.concatenate([picked[k, pl.ds(4 * h + m, RANKS, stride=8), :] for h in range(2)], axis=1)
                 for m in range(4)
             )
             for ri, values in enumerate(((u_re, u_im, v_re, v_im), (-u_im, u_re, -v_im, v_re))):
@@ -365,6 +366,7 @@
         scale = norm / (NEV * math.sqrt(SPIN * NEV))
         nn = (((1,), (0,)), ((), ()))
         for k in (1, 0):
+            weigh(k)
             groups = [None] * 4
             for a in range(SPIN):
                 first = (-a % 4) * 32
@@ -392,7 +394,7 @@
             if k == 1:
                 go(swap)
 
-    mate = (space, (y + 1 - 2 * (y % 2)) * 2 + core)
+    mate = (space, mate_row(y, core) * 2 + core)
     swap = remote(foreign, other_out, swap_send.at[0], swap_recv.at[0], mate)
 
     def elementals():
@@ -454,7 +456,8 @@
     full_stage(0)
     a_z(4, 0)
     full_stage(1)
-    pick_stage()
+    pick_stage(1)
+    pick_stage(0)
     a_z(4, 1)
     rows_stage()
     waits(tau.at[pl.ds(0, 2)], push_recv.at[0])
@@ -479,7 +482,8 @@
         pair_copy(p).wait_send()
         waits(plane_in.at[p, pl.ds(0, PLANE - 1)], plane_send.at[p])
         waits(line_in.at[p, pl.ds(0, NZ - 1)], line_send.at[p])
-    waits(picked.at[:, pl.ds(0, 8 * RANKS - 8)], pick_send.at[0])
+    for k in range(2):
+        waits(picked.at[k, pl.ds(0, 8 * RANKS - 8)], pick_send.at[k])
     waits(rowed.at[pl.ds(0, RANKS - 1)], rows_send.at[0])
 
 
@@ -518,7 +522,7 @@
             pltpu.VMEM((NMOM, PLANE, 2, 8, NEV), F32),
             pltpu.VMEM((NMOM, NZ, 2, 8, NEV), F32),
             pltpu.VMEM((16, 2, NEV), F32),
-            pltpu.VMEM((RANKS, 2, 8, 128), F32),
+            pltpu.VMEM((2, RANKS, 8, 128), F32),
             pltpu.VMEM((2, RANKS * 8, 128), F32),
             pltpu.VMEM((RANKS, 4, NEV), F32),
             pltpu.VMEM((RANKS, 4, NEV), F32),
@@ -536,8 +540,8 @@
             dma((NMOM,)),
             dma((NMOM,)),
             dma((NMOM,)),
-            dma((1,)),
-            dma((1,)),
+            dma((2,)),
+            dma((2,)),
             dma((1,)),
             dma((1,)),
             dma((1,)),

time: 52.1 us -> 50.3 us (0.965)
  Pallas kernels: 51.2 us -> 49.4 us
    pallas_call x1, Pallas kernels: 50.1 us -> 48.3 us  [per_device(): pl.pallas_call(kernel, out_shape=(jax.ShapeDtypeStruct((NMOM, 2, width8,...]
where the time goes in v4:
time: 50.3 us; the launch traced here: 50.2 us
  Pallas kernels  49.4 us (98%)
  between operations  0.8 us (2%)
    pallas_call x1, Pallas kernels, per_device(): pl.pallas_call(kernel, out_shape=(jax.ShapeDtypeStruct((NMOM, 2, width8,...  48.3 us
    pallas_call x1, Pallas kernels, per_device(): pl.pallas_call(finish, out_shape=(jax.ShapeDtypeStruct(el.shape, F32), ja...  1.08 us

profile of v4, /device:TPU:1, one launch (start us, length us, event | category | flops | bytes accessed | tf_op | source)
XLA Modules:
  0.0 50.2 jit_solution(9786380483508569113)
XLA Ops:
  0.6 48.3 %shard_map.59 = (f32[2,2,8,32]{3,2,1,0:T(8,128)S(1)}, f32[2,128,128]{2,1,0:T(8,128)S(1)}, f32[2,128,128]{2,1,0:T(8,128)S(1)}) custom-call(s32[2,3]{1,0:T(2,128)} %momenta_in.1, s32[2,256]{1,0:T(2,128)} %bitcast.5, f32[2,3,256,1024]{3,2,1,0:T(8,128)} %bitcast.4, f32[2,32,1024]{2,1,0:T(8,128)} %sources_in.1), custom_call_target="tpu_custom_call" | custom-call | tf_op jit(solution)/shard_map/pallas_call | solution.py:495
  49.0 1.1 %shard_map.60 = (f32[2,2,8,32]{3,2,1,0:T(8,128)}, f32[2,128,128]{2,1,0:T(8,128)}) custom-call(f32[2,2,8,32]{3,2,1,0:T(8,128)S(1)} %get-tuple-element.7.el_ref, f32[2,128,128]{2,1,0:T(8,128)S(1)} %get-tuple-element.8.own_ref, f32[2,128,128]{2,1,0:T(8,128)S(1)} %get-tuple-element.9.other_ref), custom_call_target="tpu_custom_call" | custom-call | tf_op jit(solution)/shard_map/pallas_call | solution.py:587

commit v5 on v4

--- a/solution.py
+++ b/solution.py
@@ -44,7 +44,7 @@
 def kernel(
     momenta_in, graphs_in, eig, sources_in, el_out, own_out, other_out,
     momenta, graphs, sources, el_ref, own_ref, vec, left, trig, acc, ebuf, stage, pair_in, plane_in, line_in, full, pick, picked, rows, rowed,
-    tau_in, tau, tau_hi, tau_lo, wts, foreign,
+    tau_in, tau, tau_hi, tau_lo, foreign,
     load_sem, own_sem, pair_send, pair_recv, plane_send, plane_recv, line_send, line_recv,
     pick_send, pick_recv, rows_send, rows_recv,
     ax_send, ax_recv, az_send, az_recv, bz_send, bz_recv, bx_send, bx_recv, push_send, push_recv, swap_send, swap_recv, small_sem, out_sem,
@@ -57,9 +57,12 @@
     me = space * (2 * NY) + tile
     sites = vec.shape[3]
 
-    def at_plane(other_rank):
-        c, q = other_rank // PLANE, other_rank % PLANE
-        return ((q // NY) * NZ + z, (q % NY) * 2 + c)
+    xs = [x] + [(x + d) % NX for d in range(1, NX)]
+    ys = [y] + [(y + d) % NY for d in range(1, NY)]
+    cores = (core, 1 - core)
+
+    def plane_at(dx, dy, dc):
+        return (xs[dx] * NZ + z, ys[dy] * 2 + cores[dc])
 
     def at_z(zz):
         return (x * NZ + zz, tile)
@@ -71,6 +74,8 @@
 
     def mate_row(yy, c):
         return (yy + NY + 1 - 2 * ((yy + c) % 2)) % NY
+
+    mate_rows = [[mate_row(ys[dy], cores[dc]) for dc in range(2)] for dy in range(NY)]
 
     def remote(src, dst, send, recv, device):
         return pltpu.make_async_remote_copy(
@@ -79,19 +84,22 @@
 
     small = [
         pltpu.make_async_copy(momenta_in, momenta, small_sem.at[0]),
-        pltpu.make_async_copy(sources_in, sources, small_sem.at[1]),
+        pltpu.make_async_copy(
+            sources_in.at[:, pl.ds(pl.multiple_of((y % 2) * KDEV, KDEV), KDEV)], sources, small_sem.at[1]
+        ),
         pltpu.make_async_copy(graphs_in, graphs, small_sem.at[2]),
     ]
     for copy in small:
         copy.start()
     loads = [pltpu.make_async_copy(eig.at[:, c], vec.at[:, c], load_sem.at[c]) for c in range(NC)]
-    for load in loads:
-        load.start()
+    loads[0].start()
 
     barrier = pltpu.get_barrier_semaphore()
 
-    for j in range(1, RANKS):
-        pl.semaphore_signal(barrier, inc=1, device_id=at_plane((rank + j) % RANKS), device_id_type=MESH)
+    for dx, dy in PLANE_FAR + ((0, 0),):
+        for dc in range(2):
+            if dx or dy or dc:
+                pl.semaphore_signal(barrier, inc=1, device_id=plane_at(dx, dy, dc), device_id_type=MESH)
     for j in range(1, NZ):
         pl.semaphore_signal(barrier, inc=1, device_id=at_z((z + j) % NZ), device_id_type=MESH)
 
@@ -114,10 +122,9 @@
         jj = lax.broadcasted_iota(jnp.int32, (half, half), 0)
         col = lax.broadcasted_iota(jnp.int32, (half, half), 1)
         ones = (((jj & 3) * 128 + (jj >> 2)) == col).astype(F32).astype(BF16)
-        first = pl.multiple_of((y % 2) * KDEV, KDEV)
         for h in range(2):
             lanes = slice(h * half, (h + 1) * half)
-            value = jnp.concatenate([sources[0, pl.ds(first, KDEV), lanes], sources[1, pl.ds(first, KDEV), lanes]], axis=0)
+            value = jnp.concatenate([sources[0, :, lanes], sources[1, :, lanes]], axis=0)
             hi = value.astype(BF16)
             rest = value - hi.astype(F32)
             mid = rest.astype(BF16)
@@ -186,12 +193,14 @@
                 ref_u, ref_d = ref_up, ref_down
             go(remote(ref_u, ref_u, bz_send.at[0], bz_recv.at[0, h], at_z(z_on(1))))
             go(remote(ref_d, ref_d, bz_send.at[0], bz_recv.at[1, h], at_z(z_back(1))))
-            b_along_x(up, h)
-            b_along_x(down, NZ // 2 + h)
         else:
             waits(ref_up.at[0], bz_recv.at[0, h - 1])
             waits(ref_up.at[1], bz_recv.at[1, h - 1])
-            b_along_x(up, h)
+
+    def b_x(h):
+        b_along_x(z_back(h), h)
+        if h < NZ // 2:
+            b_along_x(z_on(h), NZ // 2 + h)
 
     def b_push(k):
         zz = z_back(k) if k <= NZ // 2 else z_on(k - NZ // 2)
@@ -270,10 +279,10 @@
         stage[p, core] += pair_in[p]
 
         for dx, dy in PLANE_FAR:
-            q = ((x + dx) % NX) * NY + (y + dy) % NY
+            q = xs[dx] * NY + ys[dy]
             remote(
                 stage.at[p, core, q], plane_in.at[p, place], plane_send.at[p], plane_recv.at[p],
-                at_plane(core * PLANE + q),
+                plane_at(dx, dy, 0),
             ).start()
         plane_in[p, place] = stage[p, core, place]
 
@@ -297,36 +306,39 @@
             full[p * 8 : p * 8 + 8, ri, :] = total[ri]
 
     def pick_stage(k):
-        def fill(d):
-            sp, tl = at_plane(d)
-            yy, cc = tl // 2, tl % 2
-            g = sp * (2 * NY) + (tl if k == 0 else mate_row(yy, cc) * 2 + cc)
+        def fill(dx, dy, dc):
+            other_core = cores[dc]
+            row = ys[dy] if k == 0 else mate_rows[dy][dc]
+            g = (xs[dx] * NZ + z) * (2 * NY) + row * 2 + other_core
+            d = other_core * PLANE + xs[dx] * NY + ys[dy]
             for m in range(2):
                 value = full[graphs[m, g]]
                 for h in range(2):
                     pick[k, d, h * 4 + m * 2 : h * 4 + m * 2 + 2, :] = value[:, h * 128 : h * 128 + 128]
+            return d
 
         here = picked.at[k, pl.ds(pl.multiple_of(rank * 8, 8), 8)]
         for dx, dy in PLANE_FAR + ((0, 0),):
-            for cc in (core, 1 - core):
-                if (dx, dy) == (0, 0) and cc is core:
-                    continue
-                d = cc * PLANE + ((x + dx) % NX) * NY + (y + dy) % NY
-                fill(d)
-                remote(pick.at[k, d], here, pick_send.at[k], pick_recv.at[k], at_plane(d)).start()
-        fill(rank)
+            for dc in range(2):
+                if dx or dy or dc:
+                    d = fill(dx, dy, dc)
+                    remote(
+                        pick.at[k, d], here, pick_send.at[k], pick_recv.at[k], plane_at(dx, dy, dc)
+                    ).start()
+        fill(0, 0, 0)
         picked[k, pl.ds(pl.multiple_of(rank * 8, 8), 8), :] = pick[k, rank]
 
     def rows_stage():
-        def send_rows(j, _):
-            d = (rank + j) % RANKS
-            _, tl = at_plane(d)
-            rows[d, 0:2, :] = full[tl]
-            rows[d, 2:4, :] = full[8 + tl]
-            remote(rows.at[d], rowed.at[rank], rows_send.at[0], rows_recv.at[0], at_plane(d)).start()
-            return 0
-
-        lax.fori_loop(1, RANKS, send_rows, 0)
+        for dx, dy in PLANE_FAR + ((0, 0),):
+            for dc in range(2):
+                if dx or dy or dc:
+                    tl = ys[dy] * 2 + cores[dc]
+                    d = cores[dc] * PLANE + xs[dx] * NY + ys[dy]
+                    rows[d, 0:2, :] = full[tl]
+                    rows[d, 2:4, :] = full[8 + tl]
+                    remote(
+                        rows.at[d], rowed.at[rank], rows_send.at[0], rows_recv.at[0], plane_at(dx, dy, dc)
+                    ).start()
         rowed[rank, 0:2, :] = full[tile]
         rowed[rank, 2:4, :] = full[8 + tile]
 
@@ -339,62 +351,48 @@
 
     norm = 1.0 / (NC * sites * NSPACE * 2 * NY)
 
-    def moves(first_group):
-        row = lax.broadcasted_iota(jnp.int32, (2 * BLOCK, 2 * BLOCK), 0)
-        col = lax.broadcasted_iota(jnp.int32, (2 * BLOCK, 2 * BLOCK), 1)
-        ri, a, i = row >> 7, row & 3, (row >> 2) & 31
-        want = ri * BLOCK + ((a + first_group + ri) & 3) * 32 + i
-        return (col == want).astype(F32).astype(BF16)
-
     def final():
-        def weigh(k):
+        row = lax.broadcasted_iota(jnp.int32, (BLOCK, BLOCK), 0)
+        col = lax.broadcasted_iota(jnp.int32, (BLOCK, BLOCK), 1)
+        moves = (col == (row & 3) * 32 + (row >> 2)).astype(F32).astype(BF16)
+        scale = norm / (NEV * math.sqrt(SPIN * NEV))
+        nn = (((1,), (0,)), ((), ()))
+        for k in (1, 0):
             waits(picked.at[k, pl.ds(0, 8 * RANKS - 8)], pick_recv.at[k])
             u_re, u_im, v_re, v_im = (
                 jnp.concatenate([picked[k, pl.ds(4 * h + m, RANKS, stride=8), :] for h in range(2)], axis=1)
                 for m in range(4)
             )
-            for ri, values in enumerate(((u_re, u_im, v_re, v_im), (-u_im, u_re, -v_im, v_re))):
-                for j, value in enumerate(values):
-                    for part, half in enumerate(split(value)):
-                        wts[ri, part, k, j * 32 : j * 32 + 32, :] = half
-                        if j < 3:
-                            wts[ri, part, k, j * 32 + BLOCK : j * 32 + BLOCK + 32, :] = half
-
-        lane = lax.broadcasted_iota(jnp.int32, (1, BLOCK), 1)
-        place_of = lane >> 5
-        row_moves, col_moves = moves(0), moves(2)
-        scale = norm / (NEV * math.sqrt(SPIN * NEV))
-        nn = (((1,), (0,)), ((), ()))
-        for k in (1, 0):
-            weigh(k)
-            groups = [None] * 4
+            weights = []
+            for values in ((u_re, u_im, v_re, v_im), (-u_im, u_re, -v_im, v_re)):
+                hi, lo = split(jnp.concatenate(values, axis=0))
+                weights.append((hi, jnp.concatenate([hi, lo], axis=0)))
+            totals = []
             for a in range(SPIN):
-                first = (-a % 4) * 32
                 total = None
                 for ri in range(2):
-                    w_hi = wts[ri, 0, k, first : first + BLOCK, :]
-                    both = jnp.concatenate([w_hi, wts[ri, 1, k, first : first + BLOCK, :]], axis=0)
-                    wide = dot(tau_hi[a, ri], both)
-                    new = wide[:, :BLOCK] + wide[:, BLOCK:] + dot(tau_lo[a, ri], w_hi)
+                    hi, both = weights[ri]
+                    wide = dot(both, tau_hi[a, ri])
+                    new = wide[:BLOCK] + wide[BLOCK:] + dot(hi, tau_lo[a, ri])
                     total = new if total is None else total + new
-                for g in range(4):
-                    if groups[g] is None:
-                        groups[g] = total
-                    else:
-                        groups[g] = jnp.where(place_of == (a + g) % 4, total, groups[g])
-            uh, ul = split(jnp.concatenate([groups[0], groups[1]], axis=1))
-            vh, vl = split(jnp.concatenate([groups[2], groups[3]], axis=1))
-            c4 = dot(uh, vh, TN) + dot(uh, vl, TN) + dot(ul, vh, TN)
-            hi, lo = split(c4 * scale)
-            hi, lo = split(dot(row_moves, hi, nn) + dot(row_moves, lo, nn))
-            c4 = dot(hi, col_moves) + dot(lo, col_moves)
+                totals.append(total)
+            parts = [jnp.concatenate([t[g * 32 : g * 32 + 32] for t in totals], axis=0) for g in range(4)]
+            uh, ul = split(jnp.concatenate(parts[:2], axis=0))
+            vh, vl = split(jnp.concatenate(parts[2:], axis=0))
+            c4 = dot(uh, vh) + dot(uh, vl) + dot(ul, vh)
+            re = c4[:BLOCK, :BLOCK] - c4[BLOCK:, BLOCK:]
+            im = c4[:BLOCK, BLOCK:] + c4[BLOCK:, :BLOCK]
+            hi, lo = split(jnp.concatenate([re, im], axis=1) * scale)
+            turned = dot(moves, hi, nn) + dot(moves, lo, nn)
+            hi, lo = split(jnp.concatenate([turned[:, :BLOCK], turned[:, BLOCK:]], axis=0))
+            result = dot(hi, moves) + dot(lo, moves)
             target = foreign if k == 1 else own_ref
-            target[0] = c4[:BLOCK, :BLOCK] - c4[BLOCK:, BLOCK:]
-            target[1] = c4[:BLOCK, BLOCK:] + c4[BLOCK:, :BLOCK]
+            target[0] = result[:BLOCK]
+            target[1] = result[BLOCK:]
             if k == 1:
                 go(swap)
 
-    mate = (space, mate_row(y, core) * 2 + core)
+    mate = (space, mate_rows[0][0] * 2 + core)
     swap = remote(foreign, other_out, swap_send.at[0], swap_recv.at[0], mate)
 
     def elementals():
@@ -408,13 +406,15 @@
                 ones, rowed[:, k, :], NT, precision=lax.Precision.HIGHEST, preferred_element_type=F32
             )
 
+    loads[1].start()
     acc[...] = jnp.zeros_like(acc)
     small[0].wait()
     phases()
-    loads[0].wait()
-    gram(0, 0)
     small[1].wait()
     spread()
+    loads[0].wait()
+    loads[2].start()
+    gram(0, 0)
     small[2].wait()
     pl.semaphore_wait(barrier, RANKS - 1 + NZ - 1)
     tau_first()
@@ -425,40 +425,44 @@
     gram(0, 2)
     finish_gram(0)
     acc[...] = jnp.zeros_like(acc)
+    gram(1, 0)
+    plane_stage(0)
     b_z(1)
     a_z(0, 0)
     a_z(0, 1)
-    gram(1, 0)
-    plane_stage(0)
+    b_x(1)
     gram(1, 1)
+    gram(1, 2)
+    finish_gram(1)
+    plane_stage(1)
     b_z(2)
     a_z(1, 0)
+    a_z(1, 1)
+    b_x(2)
     b_push(0)
-    gram(1, 2)
-    finish_gram(1)
-    a_z(1, 1)
-    plane_stage(1)
+    line_stage(0)
+    a_z(2, 0)
     b_z(3)
-    a_z(2, 0)
+    b_x(3)
     b_push(1)
     b_push(5)
-    line_stage(0)
+    line_stage(1)
     a_z(2, 1)
     b_z(4)
+    b_x(4)
     a_z(3, 0)
     b_push(2)
     b_push(6)
-    line_stage(1)
     a_z(3, 1)
+    full_stage(0)
+    full_stage(1)
+    pick_stage(1)
+    pick_stage(0)
+    a_z(4, 0)
+    a_z(4, 1)
     b_push(3)
     b_push(7)
     b_push(4)
-    full_stage(0)
-    a_z(4, 0)
-    full_stage(1)
-    pick_stage(1)
-    pick_stage(0)
-    a_z(4, 1)
     rows_stage()
     waits(tau.at[pl.ds(0, 2)], push_recv.at[0])
     for a in range(SPIN):
@@ -509,7 +513,7 @@
         scratch_shapes=[
             pltpu.SMEM((NMOM, 3), jnp.int32),
             pltpu.SMEM((2, NSPACE * 2 * NY), jnp.int32),
-            pltpu.VMEM((2, 2 * KDEV, SPIN * NEV), F32),
+            pltpu.VMEM((2, KDEV, SPIN * NEV), F32),
             pltpu.VMEM((NMOM, 2, width8, 32), F32),
             pltpu.VMEM((2, BLOCK, BLOCK), F32),
             pltpu.VMEM((2, NC, NEV, sites), F32),
@@ -530,7 +534,6 @@
             pltpu.VMEM((SPIN, NSPACE, 2, KDEV, NEV), F32),
             pltpu.VMEM((SPIN, 2, NSPACE * KDEV, NEV), BF16),
             pltpu.VMEM((SPIN, 2, NSPACE * KDEV, NEV), BF16),
-            pltpu.VMEM((2, 2, 2, 7 * 32, NEV), BF16),
             pltpu.VMEM((2, BLOCK, BLOCK), F32),
             dma((NC,)),
             dma((2,)),

time: 50.3 us -> 50.9 us (1.012)
  Pallas kernels: 49.4 us -> 50 us
    pallas_call x1, Pallas kernels: 48.3 us -> 49 us  [per_device(): pl.pallas_call(kernel, out_shape=(jax.ShapeDtypeStruct((NMOM, 2, width8,...]
where the time goes in v5:
time: 50.9 us; the launch traced here: 50.8 us
  Pallas kernels  50 us (98%)
  between operations  0.8 us (2%)
    pallas_call x1, Pallas kernels, per_device(): pl.pallas_call(kernel, out_shape=(jax.ShapeDtypeStruct((NMOM, 2, width8,...  49 us
    pallas_call x1, Pallas kernels, per_device(): pl.pallas_call(finish, out_shape=(jax.ShapeDtypeStruct(el.shape, F32), ja...  1.08 us

profile of v5, /device:TPU:1, one launch (start us, length us, event | category | flops | bytes accessed | tf_op | source)
XLA Modules:
  0.0 50.8 jit_solution(477603890469303418)
XLA Ops:
  0.6 49.0 %shard_map.59 = (f32[2,2,8,32]{3,2,1,0:T(8,128)S(1)}, f32[2,128,128]{2,1,0:T(8,128)S(1)}, f32[2,128,128]{2,1,0:T(8,128)S(1)}) custom-call(s32[2,3]{1,0:T(2,128)} %momenta_in.1, s32[2,256]{1,0:T(2,128)} %bitcast.5, f32[2,3,256,1024]{3,2,1,0:T(8,128)} %bitcast.4, f32[2,32,1024]{2,1,0:T(8,128)} %sources_in.1), custom_call_target="tpu_custom_call" | custom-call | tf_op jit(solution)/shard_map/pallas_call | solution.py:499
  49.6 1.1 %shard_map.60 = (f32[2,2,8,32]{3,2,1,0:T(8,128)}, f32[2,128,128]{2,1,0:T(8,128)}) custom-call(f32[2,2,8,32]{3,2,1,0:T(8,128)S(1)} %get-tuple-element.7.el_ref, f32[2,128,128]{2,1,0:T(8,128)S(1)} %get-tuple-element.8.own_ref, f32[2,128,128]{2,1,0:T(8,128)S(1)} %get-tuple-element.9.other_ref), custom_call_target="tpu_custom_call" | custom-call | tf_op jit(solution)/shard_map/pallas_call | solution.py:590

commit v6 on v5

--- a/solution.py
+++ b/solution.py
@@ -425,32 +425,32 @@
     gram(0, 2)
     finish_gram(0)
     acc[...] = jnp.zeros_like(acc)
+    a_z(0, 0)
+    a_z(0, 1)
     gram(1, 0)
     plane_stage(0)
     b_z(1)
-    a_z(0, 0)
-    a_z(0, 1)
     b_x(1)
     gram(1, 1)
     gram(1, 2)
     finish_gram(1)
+    a_z(1, 0)
     plane_stage(1)
+    a_z(1, 1)
     b_z(2)
-    a_z(1, 0)
-    a_z(1, 1)
     b_x(2)
     b_push(0)
     line_stage(0)
     a_z(2, 0)
     b_z(3)
     b_x(3)
+    a_z(2, 1)
+    line_stage(1)
     b_push(1)
     b_push(5)
-    line_stage(1)
-    a_z(2, 1)
+    a_z(3, 0)
     b_z(4)
     b_x(4)
-    a_z(3, 0)
     b_push(2)
     b_push(6)
     a_z(3, 1)

time: 50.9 us -> 49.9 us (0.980)
  Pallas kernels: 50 us -> 49 us
    pallas_call x1, Pallas kernels: 49 us -> 47.9 us  [per_device(): pl.pallas_call(kernel, out_shape=(jax.ShapeDtypeStruct((NMOM, 2, width8,...]
where the time goes in v6:
time: 49.9 us; the launch traced here: 49.8 us
  Pallas kernels  49 us (98%)
  between operations  0.8 us (2%)
    pallas_call x1, Pallas kernels, per_device(): pl.pallas_call(kernel, out_shape=(jax.ShapeDtypeStruct((NMOM, 2, width8,...  47.9 us
    pallas_call x1, Pallas kernels, per_device(): pl.pallas_call(finish, out_shape=(jax.ShapeDtypeStruct(el.shape, F32), ja...  1.08 us

profile of v6, /device:TPU:1, one launch (start us, length us, event | category | flops | bytes accessed | tf_op | source)
XLA Modules:
  0.0 49.8 jit_solution(5196177066484189702)
XLA Ops:
  0.6 47.9 %shard_map.59 = (f32[2,2,8,32]{3,2,1,0:T(8,128)S(1)}, f32[2,128,128]{2,1,0:T(8,128)S(1)}, f32[2,128,128]{2,1,0:T(8,128)S(1)}) custom-call(s32[2,3]{1,0:T(2,128)} %momenta_in.1, s32[2,256]{1,0:T(2,128)} %bitcast.5, f32[2,3,256,1024]{3,2,1,0:T(8,128)} %bitcast.4, f32[2,32,1024]{2,1,0:T(8,128)} %sources_in.1), custom_call_target="tpu_custom_call" | custom-call | tf_op jit(solution)/shard_map/pallas_call | solution.py:499
  48.6 1.1 %shard_map.60 = (f32[2,2,8,32]{3,2,1,0:T(8,128)}, f32[2,128,128]{2,1,0:T(8,128)}) custom-call(f32[2,2,8,32]{3,2,1,0:T(8,128)S(1)} %get-tuple-element.7.el_ref, f32[2,128,128]{2,1,0:T(8,128)S(1)} %get-tuple-element.8.own_ref, f32[2,128,128]{2,1,0:T(8,128)S(1)} %get-tuple-element.9.other_ref), custom_call_target="tpu_custom_call" | custom-call | tf_op jit(solution)/shard_map/pallas_call | solution.py:590
